TPU v7x, 32 devices: a whole 2x2x4 slice. The times are simulated.
32 devices in a mesh: band: 2 (over y), gx: 8 (over z, x), gy: 2 (over core).
Axes of the slice: x: 2, y: 2, z: 4, core: 2. Of those that a mesh axis runs over, the one named last changes fastest.
Arguments:
- series: float32 [32768, 256], P(('band', 'gx', 'gy')), parts along dimension 0, may hold values from -6 to 6
- templates: bfloat16 [16, 2, 128], replicated, may hold values from -0.125 to 0.125
- drift: int32 [16], replicated, may hold values from 0 to 127, as said below
Outputs:
- band_power: float32 [32768, 128], P(('band', 'gx', 'gy')), parts along dimension 0
There are 2 independent parts, one for each index of `band`. A program takes and returns all parts, laid end to end along the dimension named above; an argument that names none is the same for every part. Nothing has to cross between parts.
Inputs may be any that keep to these rules, and one draw needn't show every extreme that they name: `drift`: some template has shift 0 and some has shift 128 - 1.
All inputs are finite; a program needn't handle non-finite values.
Results may differ from a plain program's by a relative error of at most 0.0011.
Values may be sent and summed in bfloat16 or wider, within the bound.
No kernel may reach another device: no remote copies, remote signals or barrier semaphores. Data moves between devices by JAX's collectives and lax.ppermute only.
A program may use at most 192 MiB of HBM per device.

v0:
```python
import math

import jax
import jax.numpy as jnp
from jax import lax
from jax.sharding import PartitionSpec as P

COLS = 2048
TEMPLATES = 16
TAPS = 128


TWO_PI = 2.0 * math.pi


def shifted_2(value, axis, steps):
    count = lax.axis_size(axis)
    leading, last = (max(0, -steps), min(count, count - steps))
    return lax.ppermute(value, axis, [(source, source + steps) for source in range(leading, last)])


def phase_table(out_count, in_count, length):
    product = (
        jnp.arange(out_count, dtype=jnp.int32)[:, None]
        * jnp.arange(in_count, dtype=jnp.int32)[None, :]
    )
    phase_angle = (product % length).astype(jnp.float32) * (-TWO_PI / length)
    return (jnp.cos(phase_angle), jnp.sin(phase_angle))


def block_table(count):
    cosine, sine = phase_table(count, count, count)
    upper = jnp.stack([cosine, -sine], axis=1)
    lower = jnp.stack([sine, cosine], axis=1)
    return jnp.stack([upper, lower])


def rotate(signal, cosine, sine):
    real_part = signal[:, 0] * cosine - signal[:, 1] * sine
    imag_part = signal[:, 0] * sine + signal[:, 1] * cosine
    return jnp.stack([real_part, imag_part], axis=1)


def transform(signal, length, turned):
    highest = lax.Precision.HIGHEST
    outer_len = 2 ** (length.bit_length() // 2)
    inner_len = length // outer_len
    stacks = signal.shape[0]
    if turned:
        across = signal.shape[2]
        shaped = signal.reshape(stacks, 2, across, outer_len, inner_len)
        section_one = jnp.einsum(
            "xpya,sykab->sxpbk", block_table(outer_len), shaped, precision=highest
        )
    else:
        across = signal.shape[3]
        shaped = signal.reshape(stacks, 2, outer_len, inner_len, across)
        section_one = jnp.einsum(
            "xpya,syabk->sxpbk", block_table(outer_len), shaped, precision=highest
        )
    cosine, sine = phase_table(outer_len, inner_len, length)
    twisted = rotate(section_one, cosine[None, :, :, None], sine[None, :, :, None])
    section_two = jnp.einsum(
        "xqyb,sypbk->sxqpk", block_table(inner_len), twisted, precision=highest
    )
    return section_two.reshape(stacks, 2, length, across)


def spread_columns(moving):
    return lax.all_to_all(moving, ("gx", "gy"), split_axis=2, concat_axis=1, tiled=True)


def spread_rows(moving):
    return lax.all_to_all(moving, ("gx", "gy"), split_axis=1, concat_axis=2, tiled=True)


def kernel_matrix(templates, drift):
    template_count = templates.shape[0]
    tap_count = templates.shape[2]
    kernel_len = 2 * tap_count
    shifted = jnp.arange(kernel_len, dtype=jnp.int32)[None, :, None] - drift[:, None, None]
    selector = (shifted == jnp.arange(tap_count, dtype=jnp.int32)[None, None, :]).astype(
        jnp.bfloat16
    )
    kernel = jnp.einsum(
        "msj,mxj->mxs", selector, templates, preferred_element_type=jnp.float32
    ).astype(jnp.bfloat16)
    padded = jnp.concatenate(
        [kernel, jnp.zeros((template_count, 2, 3 * tap_count - kernel_len + 1), jnp.bfloat16)],
        axis=2,
    )
    tiled = jnp.tile(padded, (1, 1, tap_count))[:, :, : tap_count * 3 * tap_count]
    banded = tiled.reshape(template_count, 2, tap_count, 3 * tap_count)
    band_re = jnp.transpose(banded[:, 0], (2, 0, 1))
    band_im = jnp.transpose(banded[:, 1], (2, 0, 1))
    upper = jnp.stack([band_re, band_im], axis=1)
    lower = jnp.stack([-band_im, band_re], axis=1)
    return jnp.stack([upper, lower]).reshape(2 * 3 * tap_count, 2 * template_count * tap_count)


def window_power(extended, row_start, block_rows, wide_kernel):
    row_piece = lax.dynamic_slice_in_dim(extended, row_start, block_rows + 2, axis=1)
    windows = jnp.concatenate(
        [row_piece[:, shift_idx : shift_idx + block_rows] for shift_idx in range(3)], axis=2
    )
    stacked = jnp.transpose(windows, (1, 0, 2)).reshape(block_rows, 6 * TAPS)
    response = jnp.dot(stacked, wide_kernel, preferred_element_type=jnp.float32)
    return jnp.sum(jnp.square(response.reshape(block_rows, 2 * TEMPLATES, TAPS)), axis=1)


def body(series, templates, drift):
    groups = lax.axis_size(("gx", "gy"))
    place = lax.axis_index(("gx", "gy"))
    bin_dev = series.shape[0] * series.shape[1] // 2
    total_bins = bin_dev * groups
    row_len = total_bins // COLS
    local_rows = row_len // groups
    col_block = COLS // groups
    sample_pairs = series.reshape(local_rows, COLS, 2)
    signal = jnp.stack([sample_pairs[..., 0], sample_pairs[..., 1]])[None]
    stacks = signal.shape[0]
    moved = spread_columns(signal.reshape(stacks * 2, local_rows, COLS)).reshape(
        stacks, 2, row_len, col_block
    )
    section = transform(moved, row_len, False)
    column_ids = place * col_block + jnp.arange(col_block, dtype=jnp.int32)
    product = jnp.arange(row_len, dtype=jnp.int32)[:, None] * column_ids[None, :] % total_bins
    phase_angle = product.astype(jnp.float32) * (-TWO_PI / total_bins)
    section = rotate(section, jnp.cos(phase_angle)[None], jnp.sin(phase_angle)[None])
    moved = spread_rows(section.reshape(stacks * 2, row_len, col_block)).reshape(
        stacks, 2, local_rows, COLS
    )
    section = transform(moved, COLS, True)
    flipped = section[0][:, ::-1, :]
    rolled = jnp.roll(flipped, 1, axis=1)
    row_ids = place * local_rows + jnp.arange(local_rows, dtype=jnp.int32)
    reflected_cols = jnp.where((row_ids == 0)[None, None, :], rolled, flipped)
    section = jnp.concatenate([section, reflected_cols[None]])
    stacks = 2
    moved = spread_rows(section.reshape(stacks * 2, COLS, local_rows)).reshape(stacks, 2, bin_dev)
    landed = moved[1].reshape(2, col_block, row_len)
    placed = jnp.roll(landed[:, :, ::-1], 1, axis=2).reshape(2, bin_dev)
    mirror_re = placed[0]
    mirror_im = -placed[1]
    spec_re = moved[0, 0]
    spec_im = moved[0, 1]
    even_re = 0.5 * (spec_re + mirror_re)
    even_im = 0.5 * (spec_im + mirror_im)
    odd_re = 0.5 * (spec_im - mirror_im)
    odd_im = -0.5 * (spec_re - mirror_re)
    bin_ids = place * bin_dev + jnp.arange(bin_dev, dtype=jnp.int32)
    bin_angle = bin_ids.astype(jnp.float32) * (-TWO_PI / (2 * total_bins))
    cosine = jnp.cos(bin_angle)
    sine = jnp.sin(bin_angle)
    scale = 1.0 / math.sqrt(2 * total_bins)
    real_bins = (even_re + (cosine * odd_re - sine * odd_im)) * scale
    imag_bins = (even_im + (cosine * odd_im + sine * odd_re)) * scale
    spectrum = jnp.stack([real_bins, imag_bins]).astype(jnp.bfloat16)
    head_bins = spectrum[:, : 2 * TAPS]
    tail_bins = shifted_2(head_bins, ("gx", "gy"), -1)
    row_count = bin_dev // TAPS
    extended = jnp.concatenate([spectrum, tail_bins], axis=1).reshape(2, row_count + 2, TAPS)
    wide_kernel = kernel_matrix(templates, drift)
    block_rows = math.gcd(row_count, 512)

    def block_power(row_start):
        return window_power(extended, row_start, block_rows, wide_kernel)

    starts = jnp.arange(row_count // block_rows, dtype=jnp.int32) * block_rows
    return lax.map(block_power, starts).reshape(row_count, TAPS)


def solution(mesh):
    in_specs = (P(("band", "gx", "gy"), None), P(), P())
    out_specs = P(("band", "gx", "gy"), None)
    return jax.shard_map(body, mesh=mesh, in_specs=in_specs, out_specs=out_specs, check_vma=False)
```

profile of v0, /device:TPU:16, one launch (start us, length us, event | category | flops | bytes accessed | tf_op | source)
XLA Modules:
  0.0 408.5 jit_solution(7590701678764988163)
XLA Ops:
  0.0 69.2 %reshape.628 = f32[64,2048,2]{2,1,0:T(8,128)} reshape(f32[1024,256]{1,0:T(8,128)} %param.5) | data formatting | bytes 2097152 | tf_op jit(solution)/shard_map/reshape | solution.py:119
  69.2 62.5 %slice_reduce_fusion.1 = (f32[64,2048]{1,0:T(8,128)S(1)}, f32[64,2048]{1,0:T(8,128)S(1)}) fusion(f32[64,2048,2]{2,1,0:T(8,128)} %reshape.628), kind=kLoop, calls=%fused_computation.7 | loop fusion | bytes 2097152 | tf_op jit(solution)/shard_map/slice | solution.py:120
  136.0 6.4 %all-to-all-start = ((f32[16,1,16384]{2,1,0:T(1,128)}), f32[16,1,16384]{2,1,0:T(1,128)S(1)}, u32[]{:S(2)}, u32[]{:S(2)}) async-start(f32[16,1,16384]{2,1,0:T(1,128)} %reshape.656), calls=%async_computation | async-start | bytes 2097152 | tf_op jit(solution)/shard_map/all_to_all | solution.py:70
  142.7 24.7 %all-to-all-done = f32[16,1,16384]{2,1,0:T(1,128)S(1)} async-done(((f32[16,1,16384]{2,1,0:T(1,128)}), f32[16,1,16384]{2,1,0:T(1,128)S(1)}, u32[]{:S(2)}, u32[]{:S(2)}) %all-to-all-start) | async-done | bytes 1048608 | tf_op jit(solution)/shard_map/all_to_all | solution.py:70
  182.3 5.0 %all-to-all-start.1 = ((f32[2,1024,128]{2,0,1:T(2,128)}), f32[2,1024,128]{2,0,1:T(2,128)S(1)}, u32[]{:S(2)}, u32[]{:S(2)}) async-start(f32[2,1024,128]{2,0,1:T(2,128)} %copy.93), calls=%async_computation.1 | async-start | bytes 2097152 | tf_op jit(solution)/shard_map/all_to_all | solution.py:74
  187.8 24.6 %all-to-all-done.1 = f32[2,1024,128]{2,0,1:T(2,128)S(1)} async-done(((f32[2,1024,128]{2,0,1:T(2,128)}), f32[2,1024,128]{2,0,1:T(2,128)S(1)}, u32[]{:S(2)}, u32[]{:S(2)}) %all-to-all-start.1) | async-done | bytes 1048608 | tf_op jit(solution)/shard_map/all_to_all | solution.py:74
  213.1 4.3 %fusion.3 = f32[1,2,64,32,64]{2,4,1,3,0:T(8,128)S(1)} fusion(f32[2,64,64,32,1]{1,3,2,0,4:T(8,128)S(1)} %bitcast.184, f32[1,64,2,64]{3,1,2,0:T(8,128)S(1)} %get-tuple-element.86, f32[1,64,2,64]{3,1,2,0:T(8,128)S(1)} %get-tuple-element.85), kind=kOutput, calls=%fused_computation.19 | convolution fusion | flops 402669568 | bytes 2162688 | tf_op jit(solution)/shard_map/xpya,sykab->sxpbk/dot_general | solution.py:52
  222.6 3.4 convolution_bitcast_fusion
  231.2 6.0 %rev.4 = f32[2,2048,64]{1,2,0:T(8,128)} reverse(f32[2,2048,64]{1,2,0:T(8,128)S(1)} %squeeze_reshape.3), dimensions={1} | reverse | bytes 2097152 | tf_op jit(solution)/shard_map/rev | solution.py:134
  237.9 9.4 %reverse.4 = f32[2,2048,64]{1,2,0:T(8,128)} reverse(f32[2,2048,64]{1,2,0:T(8,128)} %bitcast.192), dimensions={1} | reverse | bytes 2097152
  252.6 6.7 %reshape.658 = f32[16,1,32768]{2,1,0:T(1,128)} reshape(f32[2048,4,64]{2,1,0:T(4,128)} %bitcast.174) | data formatting | bytes 4194304
  259.3 4.7 %all-to-all-start.2 = ((f32[16,1,32768]{2,1,0:T(1,128)}), f32[16,1,32768]{2,1,0:T(1,128)}, u32[]{:S(2)}, u32[]{:S(2)}) async-start(f32[16,1,32768]{2,1,0:T(1,128)} %reshape.658), calls=%async_computation.2 | async-start | bytes 4194304 | tf_op jit(solution)/shard_map/all_to_all | solution.py:74
  267.3 6.4 %tile.10 = bf16[16,2,49280]{2,0,1:T(8,128)(2,1)S(1)} reshape(bf16[16,2,128,385]{3,2,0,1:T(8,128)(2,1)} %tile.4) | data formatting | bytes 6307840 | tf_op jit(solution)/shard_map/tile | solution.py:92
  284.4 27.3 %all-to-all-done.2 = f32[16,1,32768]{2,1,0:T(1,128)} async-done(((f32[16,1,32768]{2,1,0:T(1,128)}), f32[16,1,32768]{2,1,0:T(1,128)}, u32[]{:S(2)}, u32[]{:S(2)}) %all-to-all-start.2) | async-done | bytes 2097184 | tf_op jit(solution)/shard_map/all_to_all | solution.py:74
  311.7 7.5 %reduce.5 = f32[16,32768]{1,0:T(8,128)S(1)} reduce(f32[16,1,32768]{2,1,0:T(1,128)} %all-to-all-done.2, f32[]{:T(128)} %broadcast.669), dimensions={1}, to_apply=%all_to_all.39.reduce_sub_computation | reduce | bytes 4194308 | tf_op jit(solution)/shard_map/all_to_all | solution.py:74
  319.3 4.3 %reshape.659 = f32[2048,4,64]{2,1,0:T(4,128)} reshape(f32[16,32768]{1,0:T(8,128)S(1)} %reduce.5) | data formatting | bytes 4194304
  328.9 4.5 %copy.149 = f32[4,16,128,64]{3,1,2,0:T(8,128)} copy(f32[4,16,128,64]{3,0,2,1:T(4,128)S(1)} %bitcast.173) | data formatting | bytes 4194304 | tf_op jit(solution)/shard_map/all_to_all | solution.py:74
  337.6 3.7 reshape.637
  341.4 19.2 %multiply_convert_fusion.1 = (bf16[1,131072]{1,0:T(2,128)(2,1)S(1)}, bf16[1,131072]{1,0:T(2,128)(2,1)S(1)}) fusion(f32[1,131072]{1,0:T(1,128)} %bitcast.197, f32[1,131072]{1,0:T(1,128)} %bitcast.198, f32[2,2,131072]{2,1,0:T(2,128)S(1)} %reshape.637, s32[]{:T(128)S(6)} %mul.618), kind=kLoop, calls=%fused_computation.52 | loop fusion | flops 3014656 | bytes 2621444 | tf_op jit(solution)/shard_map/convert
  363.5 10.6 %reshape.640 = bf16[768,4096]{1,0:T(8,128)(2,1)} reshape(bf16[2,384,2,16,128]{4,3,2,1,0:T(8,128)(2,1)} %pad_maximum_fusion) | data formatting | bytes 12582912 | tf_op jit(solution)/shard_map/reshape | solution.py:98
  374.1 8.6 %copy.112 = bf16[768,4096]{0,1:T(8,128)(2,1)} copy(bf16[768,4096]{1,0:T(8,128)(2,1)} %reshape.640) | data formatting | bytes 12582912 | tf_op jit(solution)/shard_map/while | solution.py:170
  385.3 22.3 %while.10 = (s32[]{:T(128)}, f32[2,512,128]{2,1,0:T(8,128)}, s32[2]{0:T(128)S(1)}, bf16[2,1026,128]{2,0,1:T(2,128)(2,1)S(1)}, bf16[768,4096]{0,1:T(8,128)(2,1)},...) while((s32[]{:T(128)}, f32[2,512,128]{2,1,0:T(8,128)}, s32[2]{0:T(128)S(1)}, ...), condition=%wide.region_2.3_spmd, body=%wide.region_0.2_spmd.sunk | while | flops 3227713536 | bytes 16777460 | solution.py:170
  389.9 5.6 %multiply_reduce_fusion.2 = f32[512,128]{1,0:T(8,128)S(1)} fusion(bf16[512,768,1]{1,0,2:T(8,128)(2,1)S(1)} %reshape.661, bf16[32,128,768]{2,1,0:T(8,128)(2,1)} %bitcast.185), kind=kOutput, calls=%fused_computation.clone.1 | convolution fusion | flops 3225354240 | bytes 7340032 | tf_op jit(solution)/shard_map/while/body/eval_jaxpr/dot_general | solution.py:107
  401.0 5.6 %multiply_reduce_fusion.2 = f32[512,128]{1,0:T(8,128)S(1)} fusion(bf16[512,768,1]{1,0,2:T(8,128)(2,1)S(1)} %reshape.661, bf16[32,128,768]{2,1,0:T(8,128)(2,1)} %bitcast.185), kind=kOutput, calls=%fused_computation.clone.1 | convolution fusion | flops 3225354240 | bytes 7340032 | tf_op jit(solution)/shard_map/while/body/eval_jaxpr/dot_general | solution.py:107
  (100 shorter events, 73.4 us)
Async XLA Ops:
  0.0 264.1 %copy-start = (bf16[16,2,128]{2,1,0:T(2,128)(2,1)S(1)}, bf16[16,2,128]{2,1,0:T(2,128)(2,1)}, u32[]{:S(2)}) copy-start(bf16[16,2,128]{2,1,0:T(2,128)(2,1)} %param.6) | copy-start | bytes 24580
  136.0 31.5 %all-to-all-start = ((f32[16,1,16384]{2,1,0:T(1,128)}), f32[16,1,16384]{2,1,0:T(1,128)S(1)}, u32[]{:S(2)}, u32[]{:S(2)}) async-start(f32[16,1,16384]{2,1,0:T(1,128)} %reshape.656), calls=%async_computation | async-start | bytes 2097152 | tf_op jit(solution)/shard_map/all_to_all | solution.py:70
  182.3 30.1 %all-to-all-start.1 = ((f32[2,1024,128]{2,0,1:T(2,128)}), f32[2,1024,128]{2,0,1:T(2,128)S(1)}, u32[]{:S(2)}, u32[]{:S(2)}) async-start(f32[2,1024,128]{2,0,1:T(2,128)} %copy.93), calls=%async_computation.1 | async-start | bytes 2097152 | tf_op jit(solution)/shard_map/all_to_all | solution.py:74
  229.9 7.3 %copy-start.3 = (f32[2,2048,64]{1,2,0:T(8,128)}, f32[2,2048,64]{1,2,0:T(8,128)S(1)}, u32[]{:S(2)}) copy-start(f32[2,2048,64]{1,2,0:T(8,128)S(1)} %squeeze_reshape.3) | copy-start | bytes 3145732
  237.9 11.0 %slice-start = ((f32[2,2048,64]{1,2,0:T(8,128)}), f32[2,1,64]{1,2,0:T(8,128)S(1)}, s32[]{:S(2)}) async-start(f32[2,2048,64]{1,2,0:T(8,128)} %copy-done.3), calls=%async_computation.3 | async-start | bytes 131072 | tf_op jit(solution)/shard_map/jit(_roll_static)/slice | solution.py:135
  237.9 11.0 %copy-start.4 = (f32[2,2048,64]{1,2,0:T(8,128)S(1)}, f32[2,2048,64]{1,2,0:T(8,128)}, u32[]{:S(2)}) copy-start(f32[2,2048,64]{1,2,0:T(8,128)} %rev.4) | copy-start | bytes 3145732
  259.3 4.7 %copy-start.5 = (s32[16]{0:T(128)S(1)}, s32[16]{0:T(128)}, u32[]{:S(2)}) copy-start(s32[16]{0:T(128)} %param.7) | copy-start | bytes 196
  259.3 52.4 %all-to-all-start.2 = ((f32[16,1,32768]{2,1,0:T(1,128)}), f32[16,1,32768]{2,1,0:T(1,128)}, u32[]{:S(2)}, u32[]{:S(2)}) async-start(f32[16,1,32768]{2,1,0:T(1,128)} %reshape.658), calls=%async_computation.2 | async-start | bytes 4194304 | tf_op jit(solution)/shard_map/all_to_all | solution.py:74
  326.7 2.2 copy-start.2
  360.6 22.2 %collective-permute-start = (bf16[2,256]{1,0:T(2,128)(2,1)S(1)}, bf16[2,256]{1,0:T(2,128)(2,1)S(1)}, u32[]{:S(2)}, u32[]{:S(2)}) collective-permute-start(bf16[2,256]{1,0:T(2,128)(2,1)S(1)} %pad_maximum_fusion.5), channel_id=1, source_target_pairs={{1,0},{2,1},{3,2},{4,3},{5,4},{6,5},{7,6},{8,7},{9,8},{10,9},{11,1... | collective-permute-start | bytes 3080 | tf_op jit(solution)/shard_map/ppermute | solution.py:19
  389.9 5.7 %copy-start.6 = (f32[2,512,128]{2,1,0:T(8,128)S(1)}, f32[2,512,128]{2,1,0:T(8,128)}, u32[]{:S(2)}) copy-start(f32[2,512,128]{2,1,0:T(8,128)} %get-tuple-element.147) | copy-start | bytes 1572868 | tf_op jit(solution)/shard_map/while
  395.6 0.8 copy-start.7
  401.0 5.7 %copy-start.6 = (f32[2,512,128]{2,1,0:T(8,128)S(1)}, f32[2,512,128]{2,1,0:T(8,128)}, u32[]{:S(2)}) copy-start(f32[2,512,128]{2,1,0:T(8,128)} %get-tuple-element.147) | copy-start | bytes 1572868 | tf_op jit(solution)/shard_map/while
  406.7 0.8 copy-start.7
  407.5 0.7 copy-start.1
where the time goes:
time: 416 us; the launch traced here: 408 us
  local copies, waits for them, and re-layouts  240 us (58%)
  waiting for transfers between devices  76.7 us (18%)
  other arithmetic  45.1 us (11%)
  matrix products  23.3 us (6%)
  starting transfers between devices  19 us (5%)
    reshape x1, local copies, waits for them, and re-layouts, body(): sample_pairs = series.reshape(local_rows, COLS, 2)  69.2 us
    slice x1, local copies, waits for them, and re-layouts, body(): signal = jnp.stack([sample_pairs[..., 0], sample_pairs[..., 1]])[None]  62.5 us
    all_to_all x2, waiting for transfers between devices, spread_rows(): lax.all_to_all(moving, ('gx', 'gy'), split_axis=1, concat_axis=2, tiled=T...  51.9 us
    unnamed x24, local copies, waits for them, and re-layouts  36.1 us
    all_to_all x1, waiting for transfers between devices, spread_columns(): lax.all_to_all(moving, ('gx', 'gy'), split_axis=2, concat_axis=1, tiled=T...  24.7 us
    another operation x3, other arithmetic  20.8 us
    dot_general x2, matrix products, window_power(): response = jnp.dot(stacked, wide_kernel, preferred_element_type=jnp.float32)  11.3 us
    reshape x1, local copies, waits for them, and re-layouts, kernel_matrix(): jnp.stack([upper, lower])  10.6 us
  transfers between devices with their start and end apart: 4, of which 3 were waited for; matrix products, arithmetic and copies ran while one was open for 10% of the time, Pallas kernels for 0%

commit v1 on v0

v1 whole, which is shorter than its diff:
```python
import math

import jax
import jax.numpy as jnp
import numpy as np
from jax import lax
from jax.experimental import pallas as pl
from jax.experimental.pallas import tpu as pltpu
from jax.sharding import PartitionSpec as P

LANES = 128
AXES = ("gx", "gy")
VMEM_SPEC = pl.BlockSpec(memory_space=pltpu.VMEM)
SMEM_SPEC = pl.BlockSpec(memory_space=pltpu.SMEM)
F32 = jnp.float32
BF16 = jnp.bfloat16


def split_pair(table):
    high = np.asarray(table, np.float32).astype(BF16)
    low = (np.asarray(table, np.float64) - high.astype(np.float64)).astype(BF16)
    return high, low


def phases(product, length):
    angle = (product % length).astype(np.float64) * (-2.0 * np.pi / length)
    return np.cos(angle), np.sin(angle)


def first_matrix():
    index = np.arange(LANES, dtype=np.int64)
    real, imag = phases(index[:, None] * index[None, :], LANES)
    high, low = split_pair(np.concatenate([real, imag], axis=0))
    return np.concatenate([high, high, low], axis=1)


def second_matrix():
    index = np.arange(LANES, dtype=np.int64)
    real, imag = phases(index[:, None] * index[None, :], LANES)
    top = np.concatenate([real, -imag], axis=1)
    bottom = np.concatenate([imag, real], axis=1)
    high, low = split_pair(np.concatenate([top, bottom], axis=0))
    return np.concatenate([high, high, low], axis=1)


def table_pair(product, length):
    return np.stack(phases(product, length)).astype(np.float32)


def times(left, right):
    return (
        left[0] * right[0] - left[1] * right[1],
        left[0] * right[1] + left[1] * right[0],
    )


def small_fft(values):
    count = len(values)
    if count == 1:
        return values
    even = small_fft(values[0::2])
    odd = small_fft(values[1::2])
    head, tail = [], []
    for step in range(count // 2):
        real, imag = odd[step]
        if step == 0:
            turned = (real, imag)
        elif 4 * step == count:
            turned = (imag, -real)
        elif 8 * step == count:
            turned = ((real + imag) * math.sqrt(0.5), (imag - real) * math.sqrt(0.5))
        elif 8 * step == 3 * count:
            turned = ((imag - real) * math.sqrt(0.5), (real + imag) * -math.sqrt(0.5))
        else:
            angle = -2.0 * math.pi * step / count
            cosine, sine = math.cos(angle), math.sin(angle)
            turned = (real * cosine - imag * sine, real * sine + imag * cosine)
        head.append((even[step][0] + turned[0], even[step][1] + turned[1]))
        tail.append((even[step][0] - turned[0], even[step][1] - turned[1]))
    return head + tail


def powered(first, count):
    powers = [None, first]
    for step in range(2, count):
        half = step // 2
        powers.append(times(powers[half], powers[step - half]))
    return powers


def columns_kernel(groups, series_ref, out_ref, turned):
    rows, width = series_ref.shape
    per_row = width // groups
    tall = rows // LANES
    for high in range(tall):
        turned[...] = series_ref[high * LANES : (high + 1) * LANES, :].T
        for dest in range(groups):
            out_ref[dest, pl.ds(high, per_row, stride=tall), :] = turned[
                pl.ds(dest, per_row, stride=groups), :
            ]


def spread_samples(series, groups):
    rows, width = series.shape
    per_row = width // groups
    inner = rows * width // (LANES * LANES)
    tall = LANES // groups
    if per_row == inner:
        return pl.pallas_call(
            lambda *refs: columns_kernel(groups, *refs),
            out_shape=jax.ShapeDtypeStruct((groups, inner * tall, LANES), F32),
            in_specs=[VMEM_SPEC],
            out_specs=VMEM_SPEC,
            scratch_shapes=[pltpu.VMEM((width, LANES), F32)],
        )(series)
    shaped = series.reshape(tall, LANES, inner // per_row, per_row, groups)
    return jnp.transpose(shaped, (4, 2, 3, 0, 1)).reshape(groups, inner * tall, LANES)


def local_kernel(groups, y_ref, w1_ref, w2_ref, t1_ref, t2_ref, out_ref, rhs, lhs, mid, bins, edge):
    inner = mid.shape[0]
    tall = y_ref.shape[1] // inner
    own = out_ref.shape[1] // 2 - 4
    for pair in range(inner // 2):
        for part in range(2):
            step = 2 * pair + part
            block = y_ref[:, step * tall : (step + 1) * tall, :].reshape(LANES, LANES)
            high = block.astype(BF16)
            low = (block - high.astype(F32)).astype(BF16)
            cols = slice(part * LANES, (part + 1) * LANES)
            rhs[0:LANES, cols] = high
            rhs[LANES : 2 * LANES, cols] = low
            rhs[2 * LANES : 3 * LANES, cols] = high
        first = jnp.dot(w1_ref[...], rhs[...], preferred_element_type=F32)
        for part in range(2):
            cols = slice(part * LANES, (part + 1) * LANES)
            turned = times(
                (first[:LANES, cols], first[LANES:, cols]), (t1_ref[0], t1_ref[1])
            )
            rows = slice(part * LANES, (part + 1) * LANES)
            for comp in range(2):
                high = turned[comp].astype(BF16)
                low = (turned[comp] - high.astype(F32)).astype(BF16)
                at = comp * LANES
                lhs[rows, at : at + LANES] = high
                lhs[rows, 2 * LANES + at : 3 * LANES + at] = low
                lhs[rows, 4 * LANES + at : 5 * LANES + at] = high
        second = lax.dot_general(
            w2_ref[...], lhs[...], (((1,), (1,)), ((), ())), preferred_element_type=F32
        )
        mid[2 * pair] = second[:, :LANES]
        mid[2 * pair + 1] = second[:, LANES:]

    def combine(chunk, carry):
        rows = pl.ds(pl.multiple_of(chunk * 8, 8), 8)
        rows_im = pl.ds(pl.multiple_of(LANES + chunk * 8, 8), 8)
        powers = powered((t2_ref[0, rows, :], t2_ref[1, rows, :]), inner)
        values = [(mid[0, rows, :], mid[0, rows_im, :])]
        for step in range(1, inner):
            values.append(times((mid[step, rows, :], mid[step, rows_im, :]), powers[step]))
        result = small_fft(values)
        for comp in range(2):
            for step in range(inner // 2):
                at = pl.multiple_of(8 + step * LANES + chunk * 8, 8)
                bins[comp, pl.ds(at, 8), :] = result[step][comp]
            edge[comp, rows, :] = result[inner // 2][comp]
            edge[2 + comp, rows, :] = result[inner - 1][comp]
        return carry

    lax.fori_loop(0, LANES // 8, combine, 0)
    total = inner // 2 * LANES
    for comp in range(2):
        bins[comp, 0:8, :] = edge[2 + comp, LANES - 8 : LANES, :]
        bins[comp, 8 + total : 16 + total, :] = edge[comp, 0:8, :]
    for dest in range(groups):
        base = 8 + own * dest
        for comp in range(2):
            out_ref[dest, comp * own : (comp + 1) * own, :] = bins[comp, base : base + own, :]
            at = 2 * own + 4 * comp
            out_ref[dest, at : at + 2, :] = bins[comp, base - 2 : base, :]
            out_ref[dest, at + 2 : at + 4, :] = bins[comp, base + own : base + own + 2, :]


def local_transform(moved, groups, w1, w2, t1, t2):
    inner = moved.shape[1] * groups // LANES
    total = inner // 2 * LANES
    own = total // groups
    return pl.pallas_call(
        lambda *refs: local_kernel(groups, *refs),
        out_shape=jax.ShapeDtypeStruct((groups, 2 * own + 8, LANES), F32),
        in_specs=[VMEM_SPEC] * 5,
        out_specs=VMEM_SPEC,
        scratch_shapes=[
            pltpu.VMEM((3 * LANES, 2 * LANES), BF16),
            pltpu.VMEM((2 * LANES, 6 * LANES), BF16),
            pltpu.VMEM((inner, 2 * LANES, LANES), F32),
            pltpu.VMEM((2, total + 16, LANES), F32),
            pltpu.VMEM((4, LANES, LANES), F32),
        ],
    )(moved, w1, w2, t1, t2)


def matrix_kernel(drift_ref, taps_ref, out_ref):
    row = lax.broadcasted_iota(jnp.int32, (LANES, LANES), 0)
    col = lax.broadcasted_iota(jnp.int32, (LANES, LANES), 1)
    below = col <= row
    lag = (row - col) & (LANES - 1)

    def build(index, carry):
        shift = drift_ref[index]
        late = lag >= shift
        lane = lax.broadcasted_iota(jnp.int32, (8, LANES), 1)
        source = (-lane - shift) & (LANES - 1)
        blocks = []
        for comp in range(2):
            taps = jnp.broadcast_to(taps_ref[index, pl.ds(comp, 1), :].astype(F32), (8, LANES))
            start = jnp.take_along_axis(taps, source, axis=1)
            start = jnp.broadcast_to(start[0:1, :], (LANES, LANES))
            ring = pltpu.roll(start, 0, 1, stride=1, stride_axis=0)
            low = jnp.where(late, ring, 0.0)
            high = jnp.where(late, 0.0, ring)
            blocks.append(
                (
                    jnp.where(below, low, 0.0),
                    jnp.where(below, high, low),
                    jnp.where(below, 0.0, high),
                )
            )
        for part in range(3):
            real, imag = blocks[0][part], blocks[1][part]
            top = slice(part * LANES, (part + 1) * LANES)
            bottom = slice((3 + part) * LANES, (4 + part) * LANES)
            out_ref[index, top, 0:LANES] = real.astype(BF16)
            out_ref[index, top, LANES:] = imag.astype(BF16)
            out_ref[index, bottom, 0:LANES] = (-imag).astype(BF16)
            out_ref[index, bottom, LANES:] = real.astype(BF16)
        return carry

    lax.fori_loop(0, taps_ref.shape[0], build, 0)


def template_matrices(templates, drift):
    count = templates.shape[0]
    return pl.pallas_call(
        matrix_kernel,
        out_shape=jax.ShapeDtypeStruct((count, 6 * LANES, 2 * LANES), BF16),
        in_specs=[SMEM_SPEC, VMEM_SPEC],
        out_specs=VMEM_SPEC,
        cost_estimate=pl.CostEstimate(
            flops=count * 40 * LANES * LANES,
            bytes_accessed=count * 24 * LANES * LANES,
            transcendentals=0,
        ),
    )(drift, templates)


def power_kernel(groups, scale, place_ref, z_ref, table_ref, w_ref, out_ref, bins, lhs):
    own = z_ref.shape[1] // 2 - 4
    half = groups // 2

    def combine(chunk, carry):
        rows = pl.ds(pl.multiple_of(chunk * 8, 8), 8)
        rows_im = pl.ds(pl.multiple_of(own + chunk * 8, 8), 8)
        at = pl.ds(pl.multiple_of(8 + chunk * 8, 8), 8)
        powers = powered((table_ref[0, at, :], table_ref[1, at, :]), groups)
        values = [(z_ref[0, rows, :], z_ref[0, rows_im, :])]
        for step in range(1, groups):
            values.append(times((z_ref[step, rows, :], z_ref[step, rows_im, :]), powers[step]))
        result = small_fft(values)
        for step in range(groups):
            sign = scale if step < half else -scale
            bins[step, 0, at, :] = result[step][0] * scale
            bins[step, 1, at, :] = result[step][1] * sign
        return carry

    lax.fori_loop(0, own // 8, combine, 0)
    rim = []
    for comp in range(2):
        rim.append(
            jnp.concatenate(
                [
                    table_ref[comp, 6:8, :],
                    table_ref[comp, 8 + own : 10 + own, :],
                    table_ref[comp, 6:8, :],
                    table_ref[comp, 8 + own : 10 + own, :],
                ]
            )
        )
    powers = powered((rim[0], rim[1]), groups)
    values = []
    for step in range(groups):
        both = z_ref[step, 2 * own : 2 * own + 8, :]
        value = (both, pltpu.roll(both, 4, 0))
        values.append(times(value, powers[step]) if step else value)
    result = small_fft(values)
    for step in range(groups):
        sign = scale if step < half else -scale
        for comp in range(2):
            value = result[step][comp] * (sign if comp else scale)
            bins[step, comp, 6:8, :] = value[0:2, :]
            bins[step, comp, 8 + own : 10 + own, :] = value[2:4, :]

    lane = lax.broadcasted_iota(jnp.int32, (8, LANES), 1)
    source = (LANES - lane) & (LANES - 1)
    rank = lax.broadcasted_iota(jnp.int32, (8, LANES), 0)
    for step in range(half, groups):
        for comp in range(2):
            for chunk in range(own // 8 + 1):
                here = bins[step, comp, 8 * chunk : 8 * chunk + 8, :]
                after = bins[step, comp, 8 * chunk + 1 : 8 * chunk + 9, :]
                value = jnp.where(lane == 0, after, jnp.take_along_axis(here, source, axis=1))
                if step == half and chunk == 0:
                    value = jnp.where(place_ref[0] == 0, 0.0, value)
                bins[step, comp, 8 * chunk : 8 * chunk + 8, :] = value
    for step in range(groups):
        for comp in range(2):
            for shift in range(3):
                at = 8 + shift if step < half else 8 - shift
                cols = slice((3 * comp + shift) * LANES, (3 * comp + shift + 1) * LANES)
                lhs[step * own : (step + 1) * own, cols] = bins[
                    step, comp, at : at + own, :
                ].astype(BF16)

    piece = min(256, groups * own)
    out_ref[...] = jnp.zeros_like(out_ref)

    def template(index, carry):
        for block in range(groups * own // piece):
            rows = slice(block * piece, (block + 1) * piece)
            response = jnp.dot(lhs[rows, :], w_ref[index], preferred_element_type=F32)
            power = response[:, :LANES] * response[:, :LANES]
            power = power + response[:, LANES:] * response[:, LANES:]
            out_ref[rows, :] += power
        return carry

    lax.fori_loop(0, w_ref.shape[0], template, 0)


def template_powers(place, moved, table, matrices, scale):
    groups = moved.shape[0]
    own = moved.shape[1] // 2 - 4
    return pl.pallas_call(
        lambda *refs: power_kernel(groups, scale, *refs),
        out_shape=jax.ShapeDtypeStruct((groups * own, LANES), F32),
        in_specs=[SMEM_SPEC, VMEM_SPEC, VMEM_SPEC, VMEM_SPEC],
        out_specs=VMEM_SPEC,
        scratch_shapes=[
            pltpu.VMEM((groups, 2, own + 24, LANES), F32),
            pltpu.VMEM((groups * own, 6 * LANES), BF16),
        ],
    )(place, moved, table, matrices)


def place_kernel(place_ref, power_ref, out_ref):
    groups, own = power_ref.shape[0], power_ref.shape[1]
    total = groups * own
    flip = 7 - lax.broadcasted_iota(jnp.int32, (8, LANES), 0)

    @pl.when(place_ref[0] % 2 == 0)
    def _():
        for source in range(groups):
            out_ref[source * own : (source + 1) * own, :] = power_ref[source]

    @pl.when(place_ref[0] % 2 == 1)
    def _():
        for source in range(groups):
            for chunk in range(own // 8):
                at = total - source * own - 8 * chunk - 8
                value = power_ref[source, 8 * chunk : 8 * chunk + 8, :]
                out_ref[at : at + 8, :] = jnp.take_along_axis(value, flip, axis=0)


def place_powers(place, moved):
    groups, own = moved.shape[0], moved.shape[1]
    return pl.pallas_call(
        place_kernel,
        out_shape=jax.ShapeDtypeStruct((groups * own, LANES), F32),
        in_specs=[SMEM_SPEC, VMEM_SPEC],
        out_specs=VMEM_SPEC,
    )(place, moved)


def exchange(value):
    return lax.all_to_all(value, AXES, split_axis=0, concat_axis=0, tiled=True)


def body(series, templates, drift):
    groups = lax.axis_size(AXES)
    place = lax.axis_index(AXES)
    samples = series.shape[0] * series.shape[1]
    length = samples * groups
    inner = samples // (LANES * LANES)
    total = inner // 2 * LANES
    own = total // groups
    index = np.arange(LANES, dtype=np.int64)
    w1 = jnp.asarray(first_matrix())
    w2 = jnp.asarray(second_matrix())
    t1 = jnp.asarray(table_pair(index[:, None] * index[None, :], LANES * LANES))
    t2 = jnp.asarray(table_pair(LANES * index[:, None] + index[None, :], samples))
    rows = np.arange(-8, total + 8, dtype=np.int64)
    wide = jnp.asarray(table_pair(LANES * rows[:, None] + index[None, :], length))
    table = lax.dynamic_slice_in_dim(wide, place * own, own + 16, axis=1)
    place = place.astype(jnp.int32).reshape(1)

    matrices = template_matrices(templates, drift)
    moved = exchange(spread_samples(series, groups))
    partial = local_transform(moved, groups, w1, w2, t1, t2)
    moved = exchange(partial)
    power = template_powers(place, moved, table, matrices, 1.0 / math.sqrt(length))
    power = power.reshape(groups, own, LANES)
    half = groups // 2
    paired = jnp.stack([power[:half], power[half:][::-1]], axis=1)
    return place_powers(place, exchange(paired.reshape(groups, own, LANES)))


def solution(mesh):
    in_specs = (P(("band", "gx", "gy"), None), P(), P())
    out_specs = P(("band", "gx", "gy"), None)
    return jax.shard_map(body, mesh=mesh, in_specs=in_specs, out_specs=out_specs, check_vma=False)
```

time: 416 us -> 110 us (0.26)
  the two profiles are of different devices: /device:TPU:16 before, /device:TPU:0 now
where the time goes in v1:
time: 110 us
  blocking collectives  53.5 us (49%)
  Pallas kernels  31.9 us (29%)
  waiting for transfers between devices  15.8 us (14%)
  starting transfers between devices  5.03 us (5%)
  local copies, waits for them, and re-layouts  3.62 us (3%)
    all_to_all x2, blocking collectives, exchange(): return lax.all_to_all(value, AXES, split_axis=0, concat_axis=0, tiled=True)  53.5 us
    all_to_all x1, waiting for transfers between devices, exchange(): return lax.all_to_all(value, AXES, split_axis=0, concat_axis=0, tiled=True)  15.8 us
    pallas_call x1, Pallas kernels, template_powers(): pl.pallas_call(lambda *refs: power_kernel(groups, scale, *refs), out_shap...  14.1 us
    pallas_call x1, Pallas kernels, template_matrices(): pl.pallas_call(matrix_kernel, out_shape=jax.ShapeDtypeStruct((count, 6 *...  6.66 us
    pallas_call x1, Pallas kernels, local_transform(): pl.pallas_call(lambda *refs: local_kernel(groups, *refs), out_shape=jax.S...  6.3 us
    all_to_all x1, starting transfers between devices, exchange(): return lax.all_to_all(value, AXES, split_axis=0, concat_axis=0, tiled=True)  5.03 us
    pallas_call x1, Pallas kernels, spread_samples(): pl.pallas_call(lambda *refs: columns_kernel(groups, *refs), out_shape=jax...  2.91 us
  transfers between devices with their start and end apart: 1, of which 1 were waited for; matrix products, arithmetic and copies ran while one was open for 1% of the time, Pallas kernels for 6%

profile of v1, /device:TPU:0, one launch (start us, length us, event | category | flops | bytes accessed | tf_op | source)
XLA Modules:
  0.0 109.8 jit_solution(12810951254732863696)
XLA Ops:
  0.0 2.9 %shard_map.82 = f32[16,128,128]{2,1,0:T(8,128)} custom-call(f32[1024,256]{1,0:T(8,128)} %refs_0_.1), custom_call_target="tpu_custom_call" | custom-call | tf_op jit(solution)/shard_map/pallas_call | solution.py:109
  2.9 32.2 %all_to_all.15.refs_0_ = f32[16,128,128]{2,1,0:T(8,128)} all-to-all(f32[16,128,128]{2,1,0:T(8,128)} %shard_map.82), channel_id=1, replica_groups=mesh['band'=2,'gx'=8,'gy'=2] {'gx','gy'}, dimensions={0} | all-to-all | bytes 2097152 | tf_op jit(solution)/shard_map/all_to_all | solution.py:384
  35.1 6.3 %shard_map.83 = f32[16,136,128]{2,1,0:T(8,128)} custom-call(f32[16,128,128]{2,1,0:T(8,128)} %all_to_all.15.refs_0_, bf16[256,384]{1,0:T(8,128)(2,1)} %constant.26.clone.refs_1_, bf16[256,768]{1,0:T(8,128)(2,1)} %constant.27.clone.refs_2_, f32[2,128,128]{2,1,0:T(8,128)} %constant.28.clone.refs_3_, f32[2,128,128]{2,1,0:T(8,128)} %constant.29.clone.refs_4_), custom_call_target="tpu_custom_call" | custom-call | tf_op jit(solution)/shard_map/pallas_call | solution.py:188
  41.4 5.0 %all-to-all-start.1 = ((f32[16,136,128]{2,1,0:T(8,128)}), f32[16,136,128]{2,1,0:T(8,128)S(1)}, u32[]{:S(2)}, u32[]{:S(2)}) async-start(f32[16,136,128]{2,1,0:T(8,128)} %shard_map.83), calls=%async_computation.1 | async-start | bytes 2228224 | tf_op jit(solution)/shard_map/all_to_all | solution.py:384
  46.4 6.7 %shard_map.84.refs_3_ = bf16[16,768,256]{2,1,0:T(8,128)(2,1)} custom-call(s32[16]{0:T(128)} %drift_ref.1, bf16[16,2,128]{2,1,0:T(2,128)(2,1)} %taps_ref.1), custom_call_target="tpu_custom_call" | custom-call | flops 10485760 | bytes 6291456 | tf_op jit(solution)/shard_map/pallas_call | solution.py:244
  53.1 1.5 %constant_dynamic-slice_fusion.refs_2_ = f32[2,80,128]{2,1,0:T(8,128)} fusion(f32[2,1040,128]{2,1,0:T(8,128)} %constant.30.clone, s32[]{:T(128)S(6)} %select_n.3), kind=kLoop, calls=%fused_computation.2 | loop fusion | bytes 163844 | tf_op jit(solution)/shard_map/dynamic_slice | solution.py:402
  54.6 15.8 %all-to-all-done.1.refs_1_ = f32[16,136,128]{2,1,0:T(8,128)S(1)} async-done(((f32[16,136,128]{2,1,0:T(8,128)}), f32[16,136,128]{2,1,0:T(8,128)S(1)}, u32[]{:S(2)}, u32[]{:S(2)}) %all-to-all-start.1) | async-done | bytes 1114144 | tf_op jit(solution)/shard_map/all_to_all | solution.py:384
  70.4 0.0 copy-start
  70.4 1.0 copy-done
  71.4 14.1 %shard_map.85 = f32[1024,128]{1,0:T(8,128)} custom-call(s32[1]{0:T(128)} %bitcast.refs_0_.place_ref, f32[16,136,128]{2,1,0:T(8,128)} %copy-done, f32[2,80,128]{2,1,0:T(8,128)} %constant_dynamic-slice_fusion.refs_2_, bf16[16,768,256]{2,1,0:T(8,128)(2,1)} %shard_map.84.refs_3_), custom_call_target="tpu_custom_call" | custom-call | tf_op jit(solution)/shard_map/pallas_call | solution.py:342
  85.5 1.1 fusion
  86.6 21.3 %all_to_all.16.power_ref = f32[16,64,128]{2,1,0:T(8,128)} all-to-all(f32[16,64,128]{2,1,0:T(8,128)S(1)} %bitcast.8), channel_id=1, replica_groups=mesh['band'=2,'gx'=8,'gy'=2] {'gx','gy'}, dimensions={0} | all-to-all | bytes 1048576 | tf_op jit(solution)/shard_map/all_to_all | solution.py:384
  107.9 1.9 %shard_map.86 = f32[1024,128]{1,0:T(8,128)} custom-call(s32[1]{0:T(128)} %bitcast.refs_0_.place_ref, f32[16,64,128]{2,1,0:T(8,128)} %all_to_all.16.power_ref), custom_call_target="tpu_custom_call" | custom-call | tf_op jit(solution)/shard_map/pallas_call | solution.py:375
  (2 shorter events, 0.1 us)
Async XLA Ops:
  41.4 29.0 %all-to-all-start.1 = ((f32[16,136,128]{2,1,0:T(8,128)}), f32[16,136,128]{2,1,0:T(8,128)S(1)}, u32[]{:S(2)}, u32[]{:S(2)}) async-start(f32[16,136,128]{2,1,0:T(8,128)} %shard_map.83), calls=%async_computation.1 | async-start | bytes 2228224 | tf_op jit(solution)/shard_map/all_to_all | solution.py:384
  70.4 1.0 copy-start

commit v2 on v1

--- a/solution.py
+++ b/solution.py
@@ -13,6 +13,10 @@
 VMEM_SPEC = pl.BlockSpec(memory_space=pltpu.VMEM)
 SMEM_SPEC = pl.BlockSpec(memory_space=pltpu.SMEM)
 F32 = jnp.float32
+F16 = jnp.float16
+STEPS = (64, 32, 16, 8, 4, 2, 1)
+PEAK = 2.0**14
+REACH = 2.0**-40
 BF16 = jnp.bfloat16
 
 
@@ -34,9 +38,10 @@
     return np.concatenate([high, high, low], axis=1)
 
 
-def second_matrix():
+def second_matrix(gain):
     index = np.arange(LANES, dtype=np.int64)
     real, imag = phases(index[:, None] * index[None, :], LANES)
+    real, imag = real * gain, imag * gain
     top = np.concatenate([real, -imag], axis=1)
     bottom = np.concatenate([imag, real], axis=1)
     high, low = split_pair(np.concatenate([top, bottom], axis=0))
@@ -88,12 +93,35 @@
     return powers
 
 
+def grow(peak, scale):
+    code = 0.0
+    for step in STEPS:
+        grown = scale * 2.0**step
+        fits = peak * grown <= PEAK
+        scale = jnp.where(fits, grown, scale)
+        code = jnp.where(fits, code + step, code)
+    return scale, code
+
+
+def shrink(code, scale):
+    factor = jnp.full(code.shape, scale, F32)
+    for step in STEPS:
+        taken = code >= step
+        factor = jnp.where(taken, factor * 2.0**-step, factor)
+        code = jnp.where(taken, code - step, code)
+    return factor
+
+
 def columns_kernel(groups, series_ref, out_ref, turned):
     rows, width = series_ref.shape
+    scale, code = grow(jnp.max(jnp.abs(series_ref[...])), 1.0)
+    inner = out_ref.shape[1] - 8
+    for dest in range(groups):
+        out_ref[dest, inner : inner + 8, :] = jnp.full((8, LANES), code, F32)
     per_row = width // groups
     tall = rows // LANES
     for high in range(tall):
-        turned[...] = series_ref[high * LANES : (high + 1) * LANES, :].T
+        turned[...] = (series_ref[high * LANES : (high + 1) * LANES, :] * scale).T
         for dest in range(groups):
             out_ref[dest, pl.ds(high, per_row, stride=tall), :] = turned[
                 pl.ds(dest, per_row, stride=groups), :
@@ -108,23 +136,34 @@
     if per_row == inner:
         return pl.pallas_call(
             lambda *refs: columns_kernel(groups, *refs),
-            out_shape=jax.ShapeDtypeStruct((groups, inner * tall, LANES), F32),
+            out_shape=jax.ShapeDtypeStruct((groups, inner * tall + 8, LANES), F32),
             in_specs=[VMEM_SPEC],
             out_specs=VMEM_SPEC,
             scratch_shapes=[pltpu.VMEM((width, LANES), F32)],
         )(series)
-    shaped = series.reshape(tall, LANES, inner // per_row, per_row, groups)
-    return jnp.transpose(shaped, (4, 2, 3, 0, 1)).reshape(groups, inner * tall, LANES)
-
-
-def local_kernel(groups, y_ref, w1_ref, w2_ref, t1_ref, t2_ref, out_ref, rhs, lhs, mid, bins, edge):
+    scale, code = grow(jnp.max(jnp.abs(series)), F32(1.0))
+    shaped = (series * scale).reshape(tall, LANES, inner // per_row, per_row, groups)
+    moving = jnp.transpose(shaped, (4, 2, 3, 0, 1)).reshape(groups, inner * tall, LANES)
+    return jnp.concatenate([moving, jnp.full((groups, 8, LANES), code, F32)], axis=1)
+
+
+def local_kernel(
+    groups, unit, y_ref, w1_ref, w2_ref, t1_ref, t2_ref, out_ref, level_ref, rhs, lhs, mid, bins, edge
+):
     inner = mid.shape[0]
-    tall = y_ref.shape[1] // inner
+    taken = y_ref.shape[1] - 8
+    tall = taken // inner
     own = out_ref.shape[1] // 2 - 4
+    codes = y_ref[:, taken:, :]
+    least = jnp.min(codes, axis=0)
+    level_ref[...] = shrink(least, unit)
+    factor = shrink(codes - least[None], 1.0)
+    factor = factor[:, :tall, :] if tall <= 8 else factor[:, :1, :]
     for pair in range(inner // 2):
         for part in range(2):
             step = 2 * pair + part
-            block = y_ref[:, step * tall : (step + 1) * tall, :].reshape(LANES, LANES)
+            block = y_ref[:, step * tall : (step + 1) * tall, :] * factor
+            block = block.reshape(LANES, LANES)
             high = block.astype(BF16)
             low = (block - high.astype(F32)).astype(BF16)
             cols = slice(part * LANES, (part + 1) * LANES)
@@ -181,15 +220,18 @@
             out_ref[dest, at + 2 : at + 4, :] = bins[comp, base + own : base + own + 2, :]
 
 
-def local_transform(moved, groups, w1, w2, t1, t2):
-    inner = moved.shape[1] * groups // LANES
+def local_transform(moved, groups, unit, w1, w2, t1, t2):
+    inner = (moved.shape[1] - 8) * groups // LANES
     total = inner // 2 * LANES
     own = total // groups
     return pl.pallas_call(
-        lambda *refs: local_kernel(groups, *refs),
-        out_shape=jax.ShapeDtypeStruct((groups, 2 * own + 8, LANES), F32),
+        lambda *refs: local_kernel(groups, unit, *refs),
+        out_shape=(
+            jax.ShapeDtypeStruct((groups, 2 * own + 8, LANES), F32),
+            jax.ShapeDtypeStruct((8, LANES), F32),
+        ),
         in_specs=[VMEM_SPEC] * 5,
-        out_specs=VMEM_SPEC,
+        out_specs=(VMEM_SPEC, VMEM_SPEC),
         scratch_shapes=[
             pltpu.VMEM((3 * LANES, 2 * LANES), BF16),
             pltpu.VMEM((2 * LANES, 6 * LANES), BF16),
@@ -200,36 +242,25 @@
     )(moved, w1, w2, t1, t2)
 
 
-def matrix_kernel(drift_ref, taps_ref, out_ref):
+def matrix_kernel(taps_ref, out_ref):
     row = lax.broadcasted_iota(jnp.int32, (LANES, LANES), 0)
     col = lax.broadcasted_iota(jnp.int32, (LANES, LANES), 1)
     below = col <= row
-    lag = (row - col) & (LANES - 1)
 
     def build(index, carry):
-        shift = drift_ref[index]
-        late = lag >= shift
         lane = lax.broadcasted_iota(jnp.int32, (8, LANES), 1)
-        source = (-lane - shift) & (LANES - 1)
+        source = (LANES - lane) & (LANES - 1)
         blocks = []
         for comp in range(2):
             taps = jnp.broadcast_to(taps_ref[index, pl.ds(comp, 1), :].astype(F32), (8, LANES))
             start = jnp.take_along_axis(taps, source, axis=1)
             start = jnp.broadcast_to(start[0:1, :], (LANES, LANES))
             ring = pltpu.roll(start, 0, 1, stride=1, stride_axis=0)
-            low = jnp.where(late, ring, 0.0)
-            high = jnp.where(late, 0.0, ring)
-            blocks.append(
-                (
-                    jnp.where(below, low, 0.0),
-                    jnp.where(below, high, low),
-                    jnp.where(below, 0.0, high),
-                )
-            )
-        for part in range(3):
+            blocks.append((jnp.where(below, ring, 0.0), jnp.where(below, 0.0, ring)))
+        for part in range(2):
             real, imag = blocks[0][part], blocks[1][part]
             top = slice(part * LANES, (part + 1) * LANES)
-            bottom = slice((3 + part) * LANES, (4 + part) * LANES)
+            bottom = slice((2 + part) * LANES, (3 + part) * LANES)
             out_ref[index, top, 0:LANES] = real.astype(BF16)
             out_ref[index, top, LANES:] = imag.astype(BF16)
             out_ref[index, bottom, 0:LANES] = (-imag).astype(BF16)
@@ -239,24 +270,29 @@
     lax.fori_loop(0, taps_ref.shape[0], build, 0)
 
 
-def template_matrices(templates, drift):
+def template_matrices(templates):
     count = templates.shape[0]
     return pl.pallas_call(
         matrix_kernel,
-        out_shape=jax.ShapeDtypeStruct((count, 6 * LANES, 2 * LANES), BF16),
-        in_specs=[SMEM_SPEC, VMEM_SPEC],
+        out_shape=jax.ShapeDtypeStruct((count, 4 * LANES, 2 * LANES), BF16),
+        in_specs=[VMEM_SPEC],
         out_specs=VMEM_SPEC,
         cost_estimate=pl.CostEstimate(
             flops=count * 40 * LANES * LANES,
             bytes_accessed=count * 24 * LANES * LANES,
             transcendentals=0,
         ),
-    )(drift, templates)
-
-
-def power_kernel(groups, scale, place_ref, z_ref, table_ref, w_ref, out_ref, bins, lhs):
+    )(templates)
+
+
+def power_kernel(
+    place_ref, drift_ref, z_ref, level_ref, table_ref, w_ref, out_ref, bins, rim_rows, lhs, near, far
+):
+    groups = z_ref.shape[0]
     own = z_ref.shape[1] // 2 - 4
     half = groups // 2
+    main = groups * own
+    scale = level_ref[...]
 
     def combine(chunk, carry):
         rows = pl.ds(pl.multiple_of(chunk * 8, 8), 8)
@@ -268,8 +304,8 @@
             values.append(times((z_ref[step, rows, :], z_ref[step, rows_im, :]), powers[step]))
         result = small_fft(values)
         for step in range(groups):
-            sign = scale if step < half else -scale
-            bins[step, 0, at, :] = result[step][0] * scale
+            sign = level_ref[...] if step < half else -level_ref[...]
+            bins[step, 0, at, :] = result[step][0] * level_ref[...]
             bins[step, 1, at, :] = result[step][1] * sign
         return carry
 
@@ -314,64 +350,101 @@
                 bins[step, comp, 8 * chunk : 8 * chunk + 8, :] = value
     for step in range(groups):
         for comp in range(2):
-            for shift in range(3):
+            for shift in range(2):
                 at = 8 + shift if step < half else 8 - shift
-                cols = slice((3 * comp + shift) * LANES, (3 * comp + shift + 1) * LANES)
+                cols = slice((2 * comp + shift) * LANES, (2 * comp + shift + 1) * LANES)
                 lhs[step * own : (step + 1) * own, cols] = bins[
                     step, comp, at : at + own, :
                 ].astype(BF16)
-
-    piece = min(256, groups * own)
-    out_ref[...] = jnp.zeros_like(out_ref)
+                at = 8 + own + shift if step < half else 7 - shift
+                rim_rows[2 * comp + shift, step : step + 1, :] = bins[step, comp, at : at + 1, :]
+    for part in range(4):
+        lhs[main:, part * LANES : (part + 1) * LANES] = rim_rows[part].astype(BF16)
+
+    near[...] = jnp.zeros_like(near)
+    far[...] = jnp.zeros_like(far)
+    pieces = max(1, main // 512)
+    edges = [main // pieces * piece for piece in range(pieces)] + [main + groups]
 
     def template(index, carry):
-        for block in range(groups * own // piece):
-            rows = slice(block * piece, (block + 1) * piece)
+        shift = drift_ref[index]
+        for piece in range(pieces):
+            rows = slice(edges[piece], edges[piece + 1])
             response = jnp.dot(lhs[rows, :], w_ref[index], preferred_element_type=F32)
             power = response[:, :LANES] * response[:, :LANES]
             power = power + response[:, LANES:] * response[:, LANES:]
-            out_ref[rows, :] += power
+            rolled = pltpu.roll(power, (LANES - shift) & (LANES - 1), 1)
+            inside = lax.broadcasted_iota(jnp.int32, rolled.shape, 1) < LANES - shift
+            near[rows, :] += jnp.where(inside, rolled, 0.0)
+            far[rows, :] += jnp.where(inside, 0.0, rolled)
         return carry
 
     lax.fori_loop(0, w_ref.shape[0], template, 0)
-
-
-def template_powers(place, moved, table, matrices, scale):
+    peak = jnp.zeros((8, LANES), F32)
+    for step in range(groups):
+        base = step * own
+        spare = far[main + step : main + step + 1, :]
+        if step < half:
+            dest = 2 * step
+            out_ref[dest, 0:own, :] = near[base : base + own, :] + far[base + 1 : base + own + 1, :]
+            out_ref[dest, own - 1 : own, :] = near[base + own - 1 : base + own, :] + spare
+        else:
+            dest = 2 * (groups - 1 - step) + 1
+            out_ref[dest, 0:own, :] = near[base : base + own, :] + far[base - 1 : base + own - 1, :]
+            out_ref[dest, 0:1, :] = near[base : base + 1, :] + spare
+        for chunk in range(own // 8):
+            peak = jnp.maximum(peak, out_ref[dest, 8 * chunk : 8 * chunk + 8, :])
+    scale, code = grow(jnp.max(peak), REACH)
+    for dest in range(groups):
+        out_ref[dest, 0:own, :] = out_ref[dest, 0:own, :] * scale
+        out_ref[dest, own : own + 8, :] = jnp.full((8, LANES), code, F32)
+
+
+def template_powers(place, drift, moved, level, table, matrices):
     groups = moved.shape[0]
     own = moved.shape[1] // 2 - 4
+    rows = groups * own + groups
     return pl.pallas_call(
-        lambda *refs: power_kernel(groups, scale, *refs),
-        out_shape=jax.ShapeDtypeStruct((groups * own, LANES), F32),
-        in_specs=[SMEM_SPEC, VMEM_SPEC, VMEM_SPEC, VMEM_SPEC],
+        power_kernel,
+        out_shape=jax.ShapeDtypeStruct((groups, own + 8, LANES), F32),
+        in_specs=[SMEM_SPEC, SMEM_SPEC] + [VMEM_SPEC] * 4,
         out_specs=VMEM_SPEC,
         scratch_shapes=[
             pltpu.VMEM((groups, 2, own + 24, LANES), F32),
-            pltpu.VMEM((groups * own, 6 * LANES), BF16),
+            pltpu.VMEM((4, groups, LANES), F32),
+            pltpu.VMEM((rows, 4 * LANES), BF16),
+            pltpu.VMEM((rows, LANES), F32),
+            pltpu.VMEM((rows, LANES), F32),
         ],
-    )(place, moved, table, matrices)
+    )(place, drift, moved, level, table, matrices)
 
 
 def place_kernel(place_ref, power_ref, out_ref):
-    groups, own = power_ref.shape[0], power_ref.shape[1]
+    groups, own = power_ref.shape[0], power_ref.shape[1] - 8
     total = groups * own
     flip = 7 - lax.broadcasted_iota(jnp.int32, (8, LANES), 0)
 
     @pl.when(place_ref[0] % 2 == 0)
     def _():
         for source in range(groups):
-            out_ref[source * own : (source + 1) * own, :] = power_ref[source]
+            factor = shrink(power_ref[source, own:, :], 1.0 / REACH)
+            for chunk in range(own // 8):
+                at = source * own + 8 * chunk
+                value = power_ref[source, 8 * chunk : 8 * chunk + 8, :] * factor
+                out_ref[at : at + 8, :] = value
 
     @pl.when(place_ref[0] % 2 == 1)
     def _():
         for source in range(groups):
+            factor = shrink(power_ref[source, own:, :], 1.0 / REACH)
             for chunk in range(own // 8):
                 at = total - source * own - 8 * chunk - 8
-                value = power_ref[source, 8 * chunk : 8 * chunk + 8, :]
+                value = power_ref[source, 8 * chunk : 8 * chunk + 8, :] * factor
                 out_ref[at : at + 8, :] = jnp.take_along_axis(value, flip, axis=0)
 
 
 def place_powers(place, moved):
-    groups, own = moved.shape[0], moved.shape[1]
+    groups, own = moved.shape[0], moved.shape[1] - 8
     return pl.pallas_call(
         place_kernel,
         out_shape=jax.ShapeDtypeStruct((groups * own, LANES), F32),
@@ -381,7 +454,8 @@
 
 
 def exchange(value):
-    return lax.all_to_all(value, AXES, split_axis=0, concat_axis=0, tiled=True)
+    moved = lax.all_to_all(value.astype(F16), AXES, split_axis=0, concat_axis=0, tiled=True)
+    return moved.astype(F32)
 
 
 def body(series, templates, drift):
@@ -394,7 +468,7 @@
     own = total // groups
     index = np.arange(LANES, dtype=np.int64)
     w1 = jnp.asarray(first_matrix())
-    w2 = jnp.asarray(second_matrix())
+    w2 = jnp.asarray(second_matrix(2.0 / samples))
     t1 = jnp.asarray(table_pair(index[:, None] * index[None, :], LANES * LANES))
     t2 = jnp.asarray(table_pair(LANES * index[:, None] + index[None, :], samples))
     rows = np.arange(-8, total + 8, dtype=np.int64)
@@ -402,15 +476,13 @@
     table = lax.dynamic_slice_in_dim(wide, place * own, own + 16, axis=1)
     place = place.astype(jnp.int32).reshape(1)
 
-    matrices = template_matrices(templates, drift)
+    matrices = template_matrices(templates)
     moved = exchange(spread_samples(series, groups))
-    partial = local_transform(moved, groups, w1, w2, t1, t2)
+    unit = samples / 2 / math.sqrt(length)
+    partial, level = local_transform(moved, groups, unit, w1, w2, t1, t2)
     moved = exchange(partial)
-    power = template_powers(place, moved, table, matrices, 1.0 / math.sqrt(length))
-    power = power.reshape(groups, own, LANES)
-    half = groups // 2
-    paired = jnp.stack([power[:half], power[half:][::-1]], axis=1)
-    return place_powers(place, exchange(paired.reshape(groups, own, LANES)))
+    power = template_powers(place, drift, moved, level, table, matrices)
+    return place_powers(place, exchange(power))
 
 
 def solution(mesh):

time: 110 us -> 89.5 us (0.81)
  blocking collectives: 53.5 us -> 38.5 us
  waiting for transfers between devices: 15.8 us -> 7.78 us
  other arithmetic: 0.04 us -> 7.6 us
  Pallas kernels: 31.9 us -> 29.8 us
  local copies, waits for them, and re-layouts: 3.62 us -> 1.53 us
  starting transfers between devices: 5.03 us -> 3.58 us
    all_to_all x2, blocking collectives: 53.5 us -> 38.5 us  [exchange(): lax.all_to_all(value.astype(F16), AXES, split_axis=0, concat_axis=0, tile...]
    all_to_all x1, waiting for transfers between devices: 15.8 us -> 7.78 us  [exchange(): lax.all_to_all(value.astype(F16), AXES, split_axis=0, concat_axis=0, tile...]
    convert_element_type x0 -> x6, other arithmetic: none -> 7.6 us  [the longest x3 4.57 us: exchange(): value.astype(F16)]
    pallas_call x3, Pallas kernels: 27.1 us -> 24.8 us  [the longest x1 12.9 us: template_powers(): pl.pallas_call(power_kernel, out_shape=jax.ShapeDtypeStruct((groups, own...]
    all_to_all x1, starting transfers between devices: 5.03 us -> 3.58 us  [exchange(): lax.all_to_all(value.astype(F16), AXES, split_axis=0, concat_axis=0, tile...]
  transfers between devices with their start and end apart: 1 -> 1, of which waited for: 1 -> 1; matrix products, arithmetic and copies ran while one was open for 1% -> 2% of each run, Pallas kernels for 6% -> 6%
where the time goes in v2:
time: 89.5 us; the launch traced here: 88.8 us
  blocking collectives  38.5 us (43%)
  Pallas kernels  29.8 us (33%)
  waiting for transfers between devices  7.78 us (9%)
  other arithmetic  7.6 us (8%)
  starting transfers between devices  3.58 us (4%)
  local copies, waits for them, and re-layouts  1.53 us (2%)
    all_to_all x2, blocking collectives, exchange(): lax.all_to_all(value.astype(F16), AXES, split_axis=0, concat_axis=0, tile...  38.5 us
    pallas_call x1, Pallas kernels, template_powers(): pl.pallas_call(power_kernel, out_shape=jax.ShapeDtypeStruct((groups, own...  12.9 us
    all_to_all x1, waiting for transfers between devices, exchange(): lax.all_to_all(value.astype(F16), AXES, split_axis=0, concat_axis=0, tile...  7.78 us
    pallas_call x1, Pallas kernels, local_transform(): pl.pallas_call(lambda *refs: local_kernel(groups, unit, *refs), out_shape...  6.39 us
    pallas_call x1, Pallas kernels, template_matrices(): pl.pallas_call(matrix_kernel, out_shape=jax.ShapeDtypeStruct((count, 4 *...  5.46 us
    convert_element_type x3, other arithmetic, exchange(): value.astype(F16)  4.57 us
    all_to_all x1, starting transfers between devices, exchange(): lax.all_to_all(value.astype(F16), AXES, split_axis=0, concat_axis=0, tile...  3.58 us
    pallas_call x1, Pallas kernels, spread_samples(): pl.pallas_call(lambda *refs: columns_kernel(groups, *refs), out_shape=jax...  3.1 us
  transfers between devices with their start and end apart: 1, of which 1 were waited for; matrix products, arithmetic and copies ran while one was open for 2% of the time, Pallas kernels for 6%

profile of v2, /device:TPU:0, one launch (start us, length us, event | category | flops | bytes accessed | tf_op | source)
XLA Modules:
  0.0 88.8 jit_solution(865822226226042740)
XLA Ops:
  0.0 3.1 %shard_map.82 = f32[16,136,128]{2,1,0:T(8,128)} custom-call(f32[1024,256]{1,0:T(8,128)} %refs_0_.1), custom_call_target="tpu_custom_call" | custom-call | tf_op jit(solution)/shard_map/pallas_call | solution.py:137
  3.1 1.3 %convert_element_type.18 = f16[16,136,128]{2,1,0:T(8,128)(2,1)S(1)} convert(f32[16,136,128]{2,1,0:T(8,128)} %shard_map.82) | non-fusion elementwise | flops 278528 | bytes 1671168 | tf_op jit(solution)/shard_map/convert_element_type | solution.py:457
  4.4 23.9 %all_to_all.15 = f16[16,136,128]{2,1,0:T(8,128)(2,1)S(1)} all-to-all(f16[16,136,128]{2,1,0:T(8,128)(2,1)S(1)} %convert_element_type.18), channel_id=1, replica_groups=mesh['band'=2,'gx'=8,'gy'=2] {'gx','gy'}, dimensions={0} | all-to-all | bytes 1114112 | tf_op jit(solution)/shard_map/all_to_all | solution.py:457
  28.3 1.1 %convert_element_type.19.refs_0_ = f32[16,136,128]{2,1,0:T(8,128)} convert(f16[16,136,128]{2,1,0:T(8,128)(2,1)S(1)} %all_to_all.15) | non-fusion elementwise | flops 278528 | bytes 1671168 | tf_op jit(solution)/shard_map/convert_element_type | solution.py:458
  29.4 6.4 %shard_map.83 = (f32[16,136,128]{2,1,0:T(8,128)}, f32[8,128]{1,0:T(8,128)}) custom-call(f32[16,136,128]{2,1,0:T(8,128)} %convert_element_type.19.refs_0_, bf16[256,384]{1,0:T(8,128)(2,1)} %constant.26.clone.refs_1_, bf16[256,768]{1,0:T(8,128)(2,1)} %constant.27.clone.refs_2_, f32[2,128,128]{2,1,0:T(8,128)} %constant.28.clone.refs_3_, ...), custom_call_target="tpu_custom_call" | custom-call | tf_op jit(solution)/shard_map/pallas_call | solution.py:227
  35.8 2.1 %convert_element_type.20 = f16[16,136,128]{2,1,0:T(8,128)(2,1)} convert(f32[16,136,128]{2,1,0:T(8,128)} %get-tuple-element.7) | non-fusion elementwise | flops 278528 | bytes 1671168 | tf_op jit(solution)/shard_map/convert_element_type | solution.py:457
  37.9 3.6 %all-to-all-start.1 = ((f16[16,136,128]{2,1,0:T(8,128)(2,1)}), f16[16,136,128]{2,1,0:T(8,128)(2,1)S(1)}, u32[]{:S(2)}, u32[]{:S(2)}) async-start(f16[16,136,128]{2,1,0:T(8,128)(2,1)} %convert_element_type.20), calls=%async_computation.1 | async-start | bytes 1114112 | tf_op jit(solution)/shard_map/all_to_all | solution.py:457
  41.5 5.5 %shard_map.84.w_ref = bf16[16,512,256]{2,1,0:T(8,128)(2,1)} custom-call(bf16[16,2,128]{2,1,0:T(2,128)(2,1)} %taps_ref.1), custom_call_target="tpu_custom_call" | custom-call | flops 10485760 | bytes 6291456 | tf_op jit(solution)/shard_map/pallas_call | solution.py:275
  47.0 1.5 %constant_dynamic-slice_fusion.table_ref = f32[2,80,128]{2,1,0:T(8,128)} fusion(f32[2,1040,128]{2,1,0:T(8,128)} %constant.30.clone, s32[]{:T(128)S(6)} %select_n.3), kind=kLoop, calls=%fused_computation | loop fusion | bytes 163844 | tf_op jit(solution)/shard_map/dynamic_slice | solution.py:476
  48.5 7.8 %all-to-all-done.1 = f16[16,136,128]{2,1,0:T(8,128)(2,1)S(1)} async-done(((f16[16,136,128]{2,1,0:T(8,128)(2,1)}), f16[16,136,128]{2,1,0:T(8,128)(2,1)S(1)}, u32[]{:S(2)}, u32[]{:S(2)}) %all-to-all-start.1) | async-done | bytes 557088 | tf_op jit(solution)/shard_map/all_to_all | solution.py:457
  56.3 1.1 %convert_element_type.21.z_ref = f32[16,136,128]{2,1,0:T(8,128)} convert(f16[16,136,128]{2,1,0:T(8,128)(2,1)S(1)} %all-to-all-done.1) | non-fusion elementwise | flops 278528 | bytes 1671168 | tf_op jit(solution)/shard_map/convert_element_type | solution.py:458
  57.4 12.9 %shard_map.85 = f32[16,72,128]{2,1,0:T(8,128)} custom-call(s32[1]{0:T(128)} %bitcast.place_ref, s32[16]{0:T(128)} %drift_ref.1, f32[16,136,128]{2,1,0:T(8,128)} %convert_element_type.21.z_ref, f32[8,128]{1,0:T(8,128)} %get-tuple-element.8.level_ref, f32[2,80,128]{2,1,0:T(8,128)} %constant_dynamic-slice_fusion.table_ref, bf16[16,512,256]{2,1,0:T(8,128)(2,1)} %shard_map.84.w_ref), custom_call_target="tpu_custom_call" | custom-call | tf_op jit(solution)/shard_map/pallas_call | solution.py:407
  70.3 1.1 %convert_element_type.22 = f16[16,72,128]{2,1,0:T(8,128)(2,1)S(1)} convert(f32[16,72,128]{2,1,0:T(8,128)} %shard_map.85) | non-fusion elementwise | flops 147456 | bytes 884736 | tf_op jit(solution)/shard_map/convert_element_type | solution.py:457
  71.4 14.6 %all_to_all.16 = f16[16,72,128]{2,1,0:T(8,128)(2,1)S(1)} all-to-all(f16[16,72,128]{2,1,0:T(8,128)(2,1)S(1)} %convert_element_type.22), channel_id=1, replica_groups=mesh['band'=2,'gx'=8,'gy'=2] {'gx','gy'}, dimensions={0} | all-to-all | bytes 589824 | tf_op jit(solution)/shard_map/all_to_all | solution.py:457
  86.0 0.8 convert_element_type.23.power_ref
  86.9 2.0 %shard_map.86 = f32[1024,128]{1,0:T(8,128)} custom-call(s32[1]{0:T(128)} %bitcast.place_ref, f32[16,72,128]{2,1,0:T(8,128)} %convert_element_type.23.power_ref), custom_call_target="tpu_custom_call" | custom-call | tf_op jit(solution)/shard_map/pallas_call | solution.py:448
Async XLA Ops:
  37.9 18.4 %all-to-all-start.1 = ((f16[16,136,128]{2,1,0:T(8,128)(2,1)}), f16[16,136,128]{2,1,0:T(8,128)(2,1)S(1)}, u32[]{:S(2)}, u32[]{:S(2)}) async-start(f16[16,136,128]{2,1,0:T(8,128)(2,1)} %convert_element_type.20), calls=%async_computation.1 | async-start | bytes 1114112 | tf_op jit(solution)/shard_map/all_to_all | solution.py:457

commit v3 on v2

--- a/solution.py
+++ b/solution.py
@@ -17,6 +17,7 @@
 STEPS = (64, 32, 16, 8, 4, 2, 1)
 PEAK = 2.0**14
 REACH = 2.0**-40
+ROOM = pltpu.CompilerParams(vmem_limit_bytes=20 * 2**20)
 BF16 = jnp.bfloat16
 
 
@@ -139,6 +140,7 @@
             out_shape=jax.ShapeDtypeStruct((groups, inner * tall + 8, LANES), F32),
             in_specs=[VMEM_SPEC],
             out_specs=VMEM_SPEC,
+        compiler_params=ROOM,
             scratch_shapes=[pltpu.VMEM((width, LANES), F32)],
         )(series)
     scale, code = grow(jnp.max(jnp.abs(series)), F32(1.0))
@@ -232,6 +234,7 @@
         ),
         in_specs=[VMEM_SPEC] * 5,
         out_specs=(VMEM_SPEC, VMEM_SPEC),
+        compiler_params=ROOM,
         scratch_shapes=[
             pltpu.VMEM((3 * LANES, 2 * LANES), BF16),
             pltpu.VMEM((2 * LANES, 6 * LANES), BF16),
@@ -277,6 +280,7 @@
         out_shape=jax.ShapeDtypeStruct((count, 4 * LANES, 2 * LANES), BF16),
         in_specs=[VMEM_SPEC],
         out_specs=VMEM_SPEC,
+        compiler_params=ROOM,
         cost_estimate=pl.CostEstimate(
             flops=count * 40 * LANES * LANES,
             bytes_accessed=count * 24 * LANES * LANES,
@@ -409,6 +413,7 @@
         out_shape=jax.ShapeDtypeStruct((groups, own + 8, LANES), F32),
         in_specs=[SMEM_SPEC, SMEM_SPEC] + [VMEM_SPEC] * 4,
         out_specs=VMEM_SPEC,
+        compiler_params=ROOM,
         scratch_shapes=[
             pltpu.VMEM((groups, 2, own + 24, LANES), F32),
             pltpu.VMEM((4, groups, LANES), F32),
@@ -450,6 +455,7 @@
         out_shape=jax.ShapeDtypeStruct((groups * own, LANES), F32),
         in_specs=[SMEM_SPEC, VMEM_SPEC],
         out_specs=VMEM_SPEC,
+        compiler_params=ROOM,
     )(place, moved)
 
 

time: 89.5 us -> 77.9 us (0.87)
  Pallas kernels: 29.8 us -> 18.5 us
  other arithmetic: 7.6 us -> 1.18 us
  local copies, waits for them, and re-layouts: 1.53 us -> 6.3 us
  waiting for transfers between devices: 7.78 us -> 9.06 us
    unnamed x0 -> x18, local copies, waits for them, and re-layouts: none -> 5.39 us
    convert_element_type x3, other arithmetic: 4.57 us -> 0.99 us  [exchange(): value.astype(F16)]
    pallas_call x1, Pallas kernels: 12.9 us -> 10.1 us  [template_powers(): pl.pallas_call(power_kernel, out_shape=jax.ShapeDtypeStruct((groups, own...]
    convert_element_type x3, other arithmetic: 3.03 us -> 0.19 us  [exchange(): return moved.astype(F32)]
    pallas_call x1, Pallas kernels: 5.46 us -> 2.82 us  [template_matrices(): pl.pallas_call(matrix_kernel, out_shape=jax.ShapeDtypeStruct((count, 4 *...]
    pallas_call x1, Pallas kernels: 6.39 us -> 3.87 us  [local_transform(): pl.pallas_call(lambda *refs: local_kernel(groups, unit, *refs), out_shape...]
    pallas_call x1, Pallas kernels: 3.1 us -> 0.88 us  [spread_samples(): pl.pallas_call(lambda *refs: columns_kernel(groups, *refs), out_shape=jax...]
    all_to_all x1, waiting for transfers between devices: 7.78 us -> 9.06 us  [exchange(): lax.all_to_all(value.astype(F16), AXES, split_axis=0, concat_axis=0, tile...]
  transfers between devices with their start and end apart: 1 -> 1, of which waited for: 1 -> 1; matrix products, arithmetic and copies ran while one was open for 2% -> 1% of each run, Pallas kernels for 6% -> 4%
where the time goes in v3:
time: 77.9 us; the launch traced here: 77.5 us
  blocking collectives  38.6 us (50%)
  Pallas kernels  18.5 us (24%)
  waiting for transfers between devices  9.06 us (12%)
  local copies, waits for them, and re-layouts  6.3 us (8%)
  starting transfers between devices  3.58 us (5%)
  other arithmetic  1.18 us (2%)
    all_to_all x2, blocking collectives, exchange(): lax.all_to_all(value.astype(F16), AXES, split_axis=0, concat_axis=0, tile...  38.6 us
    pallas_call x1, Pallas kernels, template_powers(): pl.pallas_call(power_kernel, out_shape=jax.ShapeDtypeStruct((groups, own...  10.1 us
    all_to_all x1, waiting for transfers between devices, exchange(): lax.all_to_all(value.astype(F16), AXES, split_axis=0, concat_axis=0, tile...  9.06 us
    unnamed x18, local copies, waits for them, and re-layouts  5.39 us
    pallas_call x1, Pallas kernels, local_transform(): pl.pallas_call(lambda *refs: local_kernel(groups, unit, *refs), out_shape...  3.87 us
    all_to_all x1, starting transfers between devices, exchange(): lax.all_to_all(value.astype(F16), AXES, split_axis=0, concat_axis=0, tile...  3.58 us
    pallas_call x1, Pallas kernels, template_matrices(): pl.pallas_call(matrix_kernel, out_shape=jax.ShapeDtypeStruct((count, 4 *...  2.82 us
  transfers between devices with their start and end apart: 1, of which 1 were waited for; matrix products, arithmetic and copies ran while one was open for 1% of the time, Pallas kernels for 4%

profile of v3, /device:TPU:0, one launch (start us, length us, event | category | flops | bytes accessed | tf_op | source)
XLA Modules:
  0.0 77.5 jit_solution(15368331179233472307)
XLA Ops:
  0.0 1.2 %copy-done.2 = f32[1024,256]{1,0:T(8,128)S(1)} copy-done((f32[1024,256]{1,0:T(8,128)S(1)}, f32[1024,256]{1,0:T(8,128)}, u32[]{:S(2)}) %copy-start.2) | copy-done | bytes 1048600
  1.2 0.9 %shard_map.82 = f32[16,136,128]{2,1,0:T(8,128)S(1)} custom-call(f32[1024,256]{1,0:T(8,128)S(1)} %copy-done.2), custom_call_target="tpu_custom_call" | custom-call | tf_op jit(solution)/shard_map/pallas_call | solution.py:138
  2.1 0.1 convert_element_type.18
  2.2 0.0 copy-start.3
  2.2 0.0 copy-start.4
  2.2 0.0 copy-start.5
  2.2 0.0 copy-start.6
  2.2 24.0 %all_to_all.15 = f16[16,136,128]{2,1,0:T(8,128)(2,1)S(1)} all-to-all(f16[16,136,128]{2,1,0:T(8,128)(2,1)S(1)} %convert_element_type.18), channel_id=1, replica_groups=mesh['band'=2,'gx'=8,'gy'=2] {'gx','gy'}, dimensions={0} | all-to-all | bytes 1114112 | tf_op jit(solution)/shard_map/all_to_all | solution.py:463
  26.2 0.1 convert_element_type.19.refs_0_
  26.3 0.0 copy-done.3
  26.4 3.9 %shard_map.83 = (f32[16,136,128]{2,1,0:T(8,128)S(1)}, f32[8,128]{1,0:T(8,128)S(1)}) custom-call(f32[16,136,128]{2,1,0:T(8,128)S(1)} %convert_element_type.19.refs_0_, bf16[256,384]{1,0:T(8,128)(2,1)S(1)} %copy-done.4, bf16[256,768]{1,0:T(8,128)(2,1)S(1)} %copy-done.3, f32[2,128,128]{2,1,0:T(8,128)S(1)} %copy-done.6, f32[2,128,128]{2,1,0:T(8,128)S(1)} %copy-done.5), custom_call_target="tpu_custom_call" | custom-call | tf_op jit(solution)/shard_map/pallas_call | solution.py:229
  30.2 0.0 copy-start.7
  30.2 0.9 %convert_element_type.20 = f16[16,136,128]{2,1,0:T(8,128)(2,1)} convert(f32[16,136,128]{2,1,0:T(8,128)S(1)} %get-tuple-element.7) | non-fusion elementwise | flops 278528 | bytes 1671168 | tf_op jit(solution)/shard_map/convert_element_type | solution.py:463
  31.1 3.6 %all-to-all-start.1 = ((f16[16,136,128]{2,1,0:T(8,128)(2,1)}), f16[16,136,128]{2,1,0:T(8,128)(2,1)S(1)}, u32[]{:S(2)}, u32[]{:S(2)}) async-start(f16[16,136,128]{2,1,0:T(8,128)(2,1)} %convert_element_type.20), calls=%async_computation.1 | async-start | bytes 1114112 | tf_op jit(solution)/shard_map/all_to_all | solution.py:463
  34.7 0.0 copy-done.7
  34.7 2.8 %shard_map.84.w_ref = bf16[16,512,256]{2,1,0:T(8,128)(2,1)S(1)} custom-call(bf16[16,2,128]{2,1,0:T(2,128)(2,1)S(1)} %copy-done.7), custom_call_target="tpu_custom_call" | custom-call | flops 10485760 | bytes 6291456 | tf_op jit(solution)/shard_map/pallas_call | solution.py:278
  37.6 1.9 %copy-done = bf16[16,512,256]{2,1,0:T(8,128)(2,1)} copy-done((bf16[16,512,256]{2,1,0:T(8,128)(2,1)}, bf16[16,512,256]{2,1,0:T(8,128)(2,1)S(1)}, u32[]{:S(2)}) %copy-start) | copy-done | bytes 4194328
  39.5 0.9 %constant_dynamic-slice_fusion.table_ref = f32[2,80,128]{2,1,0:T(8,128)S(1)} fusion(f32[2,1040,128]{2,1,0:T(8,128)} %constant.30.clone, s32[]{:T(128)S(6)} %select_n.3), kind=kLoop, calls=%fused_computation | loop fusion | bytes 163844 | tf_op jit(solution)/shard_map/dynamic_slice | solution.py:482
  40.4 9.1 %all-to-all-done.1 = f16[16,136,128]{2,1,0:T(8,128)(2,1)S(1)} async-done(((f16[16,136,128]{2,1,0:T(8,128)(2,1)}), f16[16,136,128]{2,1,0:T(8,128)(2,1)S(1)}, u32[]{:S(2)}, u32[]{:S(2)}) %all-to-all-start.1) | async-done | bytes 557088 | tf_op jit(solution)/shard_map/all_to_all | solution.py:463
  49.5 0.1 convert_element_type.21.z_ref
  49.6 2.2 %copy-done.1 = bf16[16,512,256]{2,1,0:T(8,128)(2,1)S(1)} copy-done((bf16[16,512,256]{2,1,0:T(8,128)(2,1)S(1)}, bf16[16,512,256]{2,1,0:T(8,128)(2,1)}, u32[]{:S(2)}) %copy-start.1) | copy-done | bytes 4194328
  51.8 10.1 %shard_map.85 = f32[16,72,128]{2,1,0:T(8,128)S(1)} custom-call(s32[1]{0:T(128)} %bitcast.place_ref, s32[16]{0:T(128)S(1)} %copy-done.8, f32[16,136,128]{2,1,0:T(8,128)S(1)} %convert_element_type.21.z_ref, f32[8,128]{1,0:T(8,128)S(1)} %get-tuple-element.8.level_ref, f32[2,80,128]{2,1,0:T(8,128)S(1)} %constant_dynamic-slice_fusion.table_ref, ...), custom_call_target="tpu_custom_call" | custom-call | tf_op jit(solution)/shard_map/pallas_call | solution.py:411
  61.9 14.6 %all_to_all.16 = f16[16,72,128]{2,1,0:T(8,128)(2,1)S(1)} all-to-all(f16[16,72,128]{2,1,0:T(8,128)(2,1)S(1)} %convert_element_type.22), channel_id=1, replica_groups=mesh['band'=2,'gx'=8,'gy'=2] {'gx','gy'}, dimensions={0} | all-to-all | bytes 589824 | tf_op jit(solution)/shard_map/all_to_all | solution.py:463
  76.5 0.9 %shard_map.86 = f32[1024,128]{1,0:T(8,128)} custom-call(s32[1]{0:T(128)} %bitcast.place_ref, f32[16,72,128]{2,1,0:T(8,128)S(1)} %convert_element_type.23.power_ref), custom_call_target="tpu_custom_call" | custom-call | tf_op jit(solution)/shard_map/pallas_call | solution.py:453
  (10 shorter events, 0.1 us)
Async XLA Ops:
  0.0 1.2 %copy-start.2 = (f32[1024,256]{1,0:T(8,128)S(1)}, f32[1024,256]{1,0:T(8,128)}, u32[]{:S(2)}) copy-start(f32[1024,256]{1,0:T(8,128)} %refs_0_.1) | copy-start | bytes 3145732
  2.2 24.1 %copy-start.3 = (bf16[256,768]{1,0:T(8,128)(2,1)S(1)}, bf16[256,768]{1,0:T(8,128)(2,1)}, u32[]{:S(2)}) copy-start(bf16[256,768]{1,0:T(8,128)(2,1)} %constant.27.clone.refs_2_) | copy-start | bytes 1179652
  2.2 24.1 %copy-start.4 = (bf16[256,384]{1,0:T(8,128)(2,1)S(1)}, bf16[256,384]{1,0:T(8,128)(2,1)}, u32[]{:S(2)}) copy-start(bf16[256,384]{1,0:T(8,128)(2,1)} %constant.26.clone.refs_1_) | copy-start | bytes 589828
  2.2 24.1 %copy-start.5 = (f32[2,128,128]{2,1,0:T(8,128)S(1)}, f32[2,128,128]{2,1,0:T(8,128)}, u32[]{:S(2)}) copy-start(f32[2,128,128]{2,1,0:T(8,128)} %constant.29.clone.refs_4_) | copy-start | bytes 393220
  2.2 24.1 %copy-start.6 = (f32[2,128,128]{2,1,0:T(8,128)S(1)}, f32[2,128,128]{2,1,0:T(8,128)}, u32[]{:S(2)}) copy-start(f32[2,128,128]{2,1,0:T(8,128)} %constant.28.clone.refs_3_) | copy-start | bytes 393220
  30.2 4.5 %copy-start.7 = (bf16[16,2,128]{2,1,0:T(2,128)(2,1)S(1)}, bf16[16,2,128]{2,1,0:T(2,128)(2,1)}, u32[]{:S(2)}) copy-start(bf16[16,2,128]{2,1,0:T(2,128)(2,1)} %taps_ref.1) | copy-start | bytes 24580
  31.1 18.4 %all-to-all-start.1 = ((f16[16,136,128]{2,1,0:T(8,128)(2,1)}), f16[16,136,128]{2,1,0:T(8,128)(2,1)S(1)}, u32[]{:S(2)}, u32[]{:S(2)}) async-start(f16[16,136,128]{2,1,0:T(8,128)(2,1)} %convert_element_type.20), calls=%async_computation.1 | async-start | bytes 1114112 | tf_op jit(solution)/shard_map/all_to_all | solution.py:463
  37.6 2.0 %copy-start = (bf16[16,512,256]{2,1,0:T(8,128)(2,1)}, bf16[16,512,256]{2,1,0:T(8,128)(2,1)S(1)}, u32[]{:S(2)}) copy-start(bf16[16,512,256]{2,1,0:T(8,128)(2,1)S(1)} %shard_map.84.w_ref) | copy-start | bytes 12582916
  39.5 10.0 %copy-start.8 = (s32[16]{0:T(128)S(1)}, s32[16]{0:T(128)}, u32[]{:S(2)}) copy-start(s32[16]{0:T(128)} %drift_ref.1) | copy-start | bytes 196
  49.6 2.2 %copy-start.1 = (bf16[16,512,256]{2,1,0:T(8,128)(2,1)S(1)}, bf16[16,512,256]{2,1,0:T(8,128)(2,1)}, u32[]{:S(2)}) copy-start(bf16[16,512,256]{2,1,0:T(8,128)(2,1)} %copy-done) | copy-start | bytes 12582916

commit v4 on v3

--- a/solution.py
+++ b/solution.py
@@ -18,6 +18,7 @@
 PEAK = 2.0**14
 REACH = 2.0**-40
 ROOM = pltpu.CompilerParams(vmem_limit_bytes=20 * 2**20)
+WIDE = pltpu.CompilerParams(vmem_limit_bytes=50 * 2**20)
 BF16 = jnp.bfloat16
 
 
@@ -140,7 +141,7 @@
             out_shape=jax.ShapeDtypeStruct((groups, inner * tall + 8, LANES), F32),
             in_specs=[VMEM_SPEC],
             out_specs=VMEM_SPEC,
-        compiler_params=ROOM,
+            compiler_params=ROOM,
             scratch_shapes=[pltpu.VMEM((width, LANES), F32)],
         )(series)
     scale, code = grow(jnp.max(jnp.abs(series)), F32(1.0))
@@ -150,14 +151,28 @@
 
 
 def local_kernel(
-    groups, unit, y_ref, w1_ref, w2_ref, t1_ref, t2_ref, out_ref, level_ref, rhs, lhs, mid, bins, edge
+    groups,
+    unit,
+    y_ref,
+    w1_ref,
+    w2_ref,
+    t1_ref,
+    t2_ref,
+    out_ref,
+    level_ref,
+    rhs,
+    lhs,
+    mid,
+    bins,
+    edge,
 ):
     inner = mid.shape[0]
     taken = y_ref.shape[1] - 8
     tall = taken // inner
     own = out_ref.shape[1] // 2 - 4
     codes = y_ref[:, taken:, :]
-    least = jnp.min(codes, axis=0)
+    least = jnp.min(jnp.min(codes, axis=0), axis=0, keepdims=True)
+    least = jnp.broadcast_to(least, level_ref.shape)
     level_ref[...] = shrink(least, unit)
     factor = shrink(codes - least[None], 1.0)
     factor = factor[:, :tall, :] if tall <= 8 else factor[:, :1, :]
@@ -245,7 +260,7 @@
     )(moved, w1, w2, t1, t2)
 
 
-def matrix_kernel(taps_ref, out_ref):
+def matrix_kernel(taps_ref, stored_ref, out_ref, sent):
     row = lax.broadcasted_iota(jnp.int32, (LANES, LANES), 0)
     col = lax.broadcasted_iota(jnp.int32, (LANES, LANES), 1)
     below = col <= row
@@ -271,16 +286,23 @@
         return carry
 
     lax.fori_loop(0, taps_ref.shape[0], build, 0)
+    copy = pltpu.make_async_copy(out_ref, stored_ref.at[pl.ds(0, out_ref.shape[0])], sent)
+    copy.start()
+    copy.wait()
 
 
 def template_matrices(templates):
     count = templates.shape[0]
     return pl.pallas_call(
         matrix_kernel,
-        out_shape=jax.ShapeDtypeStruct((count, 4 * LANES, 2 * LANES), BF16),
+        out_shape=jax.ShapeDtypeStruct((4 * count, 4 * LANES, 2 * LANES), BF16),
         in_specs=[VMEM_SPEC],
-        out_specs=VMEM_SPEC,
-        compiler_params=ROOM,
+        out_specs=pl.BlockSpec(memory_space=pl.ANY),
+        scratch_shapes=[
+            pltpu.VMEM((count, 4 * LANES, 2 * LANES), BF16),
+            pltpu.SemaphoreType.DMA,
+        ],
+        compiler_params=WIDE,
         cost_estimate=pl.CostEstimate(
             flops=count * 40 * LANES * LANES,
             bytes_accessed=count * 24 * LANES * LANES,
@@ -290,8 +312,23 @@
 
 
 def power_kernel(
-    place_ref, drift_ref, z_ref, level_ref, table_ref, w_ref, out_ref, bins, rim_rows, lhs, near, far
+    place_ref,
+    drift_ref,
+    z_ref,
+    level_ref,
+    table_ref,
+    matrices_ref,
+    out_ref,
+    bins,
+    rim_rows,
+    lhs,
+    near,
+    far,
+    w_ref,
+    arrived,
 ):
+    fetch = pltpu.make_async_copy(matrices_ref.at[pl.ds(0, w_ref.shape[0])], w_ref, arrived)
+    fetch.start()
     groups = z_ref.shape[0]
     own = z_ref.shape[1] // 2 - 4
     half = groups // 2
@@ -370,20 +407,30 @@
     pieces = max(1, main // 512)
     edges = [main // pieces * piece for piece in range(pieces)] + [main + groups]
 
-    def template(index, carry):
-        shift = drift_ref[index]
+    fetch.wait()
+    count = w_ref.shape[0]
+    batch = math.gcd(count, 8)
+
+    def template(turn, carry):
         for piece in range(pieces):
             rows = slice(edges[piece], edges[piece + 1])
-            response = jnp.dot(lhs[rows, :], w_ref[index], preferred_element_type=F32)
-            power = response[:, :LANES] * response[:, :LANES]
-            power = power + response[:, LANES:] * response[:, LANES:]
-            rolled = pltpu.roll(power, (LANES - shift) & (LANES - 1), 1)
-            inside = lax.broadcasted_iota(jnp.int32, rolled.shape, 1) < LANES - shift
-            near[rows, :] += jnp.where(inside, rolled, 0.0)
-            far[rows, :] += jnp.where(inside, 0.0, rolled)
+            here, past = None, None
+            for member in range(batch):
+                index = turn * batch + member
+                shift = drift_ref[index]
+                response = jnp.dot(lhs[rows, :], w_ref[index], preferred_element_type=F32)
+                power = response[:, :LANES] * response[:, :LANES]
+                power = power + response[:, LANES:] * response[:, LANES:]
+                rolled = pltpu.roll(power, (LANES - shift) & (LANES - 1), 1)
+                inside = lax.broadcasted_iota(jnp.int32, rolled.shape, 1) < LANES - shift
+                kept, moved = jnp.where(inside, rolled, 0.0), jnp.where(inside, 0.0, rolled)
+                here = kept if here is None else here + kept
+                past = moved if past is None else past + moved
+            near[rows, :] += here
+            far[rows, :] += past
         return carry
 
-    lax.fori_loop(0, w_ref.shape[0], template, 0)
+    lax.fori_loop(0, count // batch, template, 0)
     peak = jnp.zeros((8, LANES), F32)
     for step in range(groups):
         base = step * own
@@ -411,15 +458,17 @@
     return pl.pallas_call(
         power_kernel,
         out_shape=jax.ShapeDtypeStruct((groups, own + 8, LANES), F32),
-        in_specs=[SMEM_SPEC, SMEM_SPEC] + [VMEM_SPEC] * 4,
+        in_specs=[SMEM_SPEC, SMEM_SPEC] + [VMEM_SPEC] * 3 + [pl.BlockSpec(memory_space=pl.ANY)],
         out_specs=VMEM_SPEC,
-        compiler_params=ROOM,
+        compiler_params=WIDE,
         scratch_shapes=[
             pltpu.VMEM((groups, 2, own + 24, LANES), F32),
             pltpu.VMEM((4, groups, LANES), F32),
             pltpu.VMEM((rows, 4 * LANES), BF16),
             pltpu.VMEM((rows, LANES), F32),
             pltpu.VMEM((rows, LANES), F32),
+            pltpu.VMEM((drift.shape[0], 4 * LANES, 2 * LANES), BF16),
+            pltpu.SemaphoreType.DMA,
         ],
     )(place, drift, moved, level, table, matrices)
 

time: 77.9 us -> 73.6 us (0.945)
  local copies, waits for them, and re-layouts: 6.3 us -> 2.17 us
    unnamed x18 -> x14, local copies, waits for them, and re-layouts: 5.39 us -> 1.26 us
    pallas_call x1, Pallas kernels: 10.1 us -> 8.01 us  [template_powers(): pl.pallas_call(power_kernel, out_shape=jax.ShapeDtypeStruct((groups, own...]
    pallas_call x1, Pallas kernels: 2.82 us -> 4.78 us  [template_matrices(): pl.pallas_call(matrix_kernel, out_shape=jax.ShapeDtypeStruct((4 * count,...]
  transfers between devices with their start and end apart: 1 -> 1, of which waited for: 1 -> 1; matrix products, arithmetic and copies ran while one was open for 1% -> 1% of each run, Pallas kernels for 4% -> 7%
where the time goes in v4:
time: 73.6 us; the launch traced here: 73.2 us
  blocking collectives  38.6 us (52%)
  Pallas kernels  18.4 us (25%)
  waiting for transfers between devices  9.05 us (12%)
  starting transfers between devices  3.58 us (5%)
  local copies, waits for them, and re-layouts  2.17 us (3%)
  other arithmetic  1.19 us (2%)
    all_to_all x2, blocking collectives, exchange(): lax.all_to_all(value.astype(F16), AXES, split_axis=0, concat_axis=0, tile...  38.6 us
    all_to_all x1, waiting for transfers between devices, exchange(): lax.all_to_all(value.astype(F16), AXES, split_axis=0, concat_axis=0, tile...  9.05 us
    pallas_call x1, Pallas kernels, template_powers(): pl.pallas_call(power_kernel, out_shape=jax.ShapeDtypeStruct((groups, own...  8.01 us
    pallas_call x1, Pallas kernels, template_matrices(): pl.pallas_call(matrix_kernel, out_shape=jax.ShapeDtypeStruct((4 * count,...  4.78 us
    pallas_call x1, Pallas kernels, local_transform(): pl.pallas_call(lambda *refs: local_kernel(groups, unit, *refs), out_shape...  3.87 us
    all_to_all x1, starting transfers between devices, exchange(): lax.all_to_all(value.astype(F16), AXES, split_axis=0, concat_axis=0, tile...  3.58 us
  transfers between devices with their start and end apart: 1, of which 1 were waited for; matrix products, arithmetic and copies ran while one was open for 1% of the time, Pallas kernels for 7%

profile of v4, /device:TPU:0, one launch (start us, length us, event | category | flops | bytes accessed | tf_op | source)
XLA Modules:
  0.0 73.2 jit_solution(14847561238781802234)
XLA Ops:
  0.0 1.2 %copy-done = f32[1024,256]{1,0:T(8,128)S(1)} copy-done((f32[1024,256]{1,0:T(8,128)S(1)}, f32[1024,256]{1,0:T(8,128)}, u32[]{:S(2)}) %copy-start) | copy-done | bytes 1048600
  1.2 0.9 %shard_map.82 = f32[16,136,128]{2,1,0:T(8,128)S(1)} custom-call(f32[1024,256]{1,0:T(8,128)S(1)} %copy-done), custom_call_target="tpu_custom_call" | custom-call | tf_op jit(solution)/shard_map/pallas_call | solution.py:139
  2.1 0.1 convert_element_type.18
  2.2 0.0 copy-start.1
  2.2 0.0 copy-start.2
  2.2 0.0 copy-start.3
  2.2 0.0 copy-start.4
  2.2 24.0 %all_to_all.15 = f16[16,136,128]{2,1,0:T(8,128)(2,1)S(1)} all-to-all(f16[16,136,128]{2,1,0:T(8,128)(2,1)S(1)} %convert_element_type.18), channel_id=1, replica_groups=mesh['band'=2,'gx'=8,'gy'=2] {'gx','gy'}, dimensions={0} | all-to-all | bytes 1114112 | tf_op jit(solution)/shard_map/all_to_all | solution.py:512
  26.2 0.1 convert_element_type.19.refs_0_
  26.3 0.0 copy-done.1
  26.3 0.0 copy-done.2
  26.3 0.0 copy-done.3
  26.4 3.9 %shard_map.83 = (f32[16,136,128]{2,1,0:T(8,128)S(1)}, f32[8,128]{1,0:T(8,128)S(1)}) custom-call(f32[16,136,128]{2,1,0:T(8,128)S(1)} %convert_element_type.19.refs_0_, bf16[256,384]{1,0:T(8,128)(2,1)S(1)} %copy-done.2, bf16[256,768]{1,0:T(8,128)(2,1)S(1)} %copy-done.1, f32[2,128,128]{2,1,0:T(8,128)S(1)} %copy-done.4, f32[2,128,128]{2,1,0:T(8,128)S(1)} %copy-done.3), custom_call_target="tpu_custom_call" | custom-call | tf_op jit(solution)/shard_map/pallas_call | solution.py:244
  30.2 0.0 copy-start.5
  30.2 0.9 %convert_element_type.20 = f16[16,136,128]{2,1,0:T(8,128)(2,1)} convert(f32[16,136,128]{2,1,0:T(8,128)S(1)} %get-tuple-element.7) | non-fusion elementwise | flops 278528 | bytes 1671168 | tf_op jit(solution)/shard_map/convert_element_type | solution.py:512
  31.1 3.6 %all-to-all-start.1 = ((f16[16,136,128]{2,1,0:T(8,128)(2,1)}), f16[16,136,128]{2,1,0:T(8,128)(2,1)S(1)}, u32[]{:S(2)}, u32[]{:S(2)}) async-start(f16[16,136,128]{2,1,0:T(8,128)(2,1)} %convert_element_type.20), calls=%async_computation.1 | async-start | bytes 1114112 | tf_op jit(solution)/shard_map/all_to_all | solution.py:512
  34.7 4.8 %shard_map.84.matrices_ref = bf16[64,512,256]{2,1,0:T(8,128)(2,1)} custom-call(bf16[16,2,128]{2,1,0:T(2,128)(2,1)S(1)} %copy-done.5), custom_call_target="tpu_custom_call" | custom-call | flops 10485760 | bytes 6291456 | tf_op jit(solution)/shard_map/pallas_call | solution.py:296
  39.5 0.0 copy-start.6
  39.5 0.9 %constant_dynamic-slice_fusion.table_ref = f32[2,80,128]{2,1,0:T(8,128)S(1)} fusion(f32[2,1040,128]{2,1,0:T(8,128)} %constant.30.clone, s32[]{:T(128)S(6)} %select_n.3), kind=kLoop, calls=%fused_computation | loop fusion | bytes 163844 | tf_op jit(solution)/shard_map/dynamic_slice | solution.py:531
  40.4 9.1 %all-to-all-done.1 = f16[16,136,128]{2,1,0:T(8,128)(2,1)S(1)} async-done(((f16[16,136,128]{2,1,0:T(8,128)(2,1)}), f16[16,136,128]{2,1,0:T(8,128)(2,1)S(1)}, u32[]{:S(2)}, u32[]{:S(2)}) %all-to-all-start.1) | async-done | bytes 557088 | tf_op jit(solution)/shard_map/all_to_all | solution.py:512
  49.5 0.1 convert_element_type.21.z_ref
  49.6 8.0 %shard_map.85 = f32[16,72,128]{2,1,0:T(8,128)S(1)} custom-call(s32[1]{0:T(128)} %bitcast.place_ref, s32[16]{0:T(128)S(1)} %copy-done.6, f32[16,136,128]{2,1,0:T(8,128)S(1)} %convert_element_type.21.z_ref, f32[8,128]{1,0:T(8,128)S(1)} %get-tuple-element.8.level_ref, f32[2,80,128]{2,1,0:T(8,128)S(1)} %constant_dynamic-slice_fusion.table_ref, ...), custom_call_target="tpu_custom_call" | custom-call | tf_op jit(solution)/shard_map/pallas_call | solution.py:458
  57.6 14.6 %all_to_all.16 = f16[16,72,128]{2,1,0:T(8,128)(2,1)S(1)} all-to-all(f16[16,72,128]{2,1,0:T(8,128)(2,1)S(1)} %convert_element_type.22), channel_id=1, replica_groups=mesh['band'=2,'gx'=8,'gy'=2] {'gx','gy'}, dimensions={0} | all-to-all | bytes 589824 | tf_op jit(solution)/shard_map/all_to_all | solution.py:512
  72.3 0.9 %shard_map.86 = f32[1024,128]{1,0:T(8,128)} custom-call(s32[1]{0:T(128)} %bitcast.place_ref, f32[16,72,128]{2,1,0:T(8,128)S(1)} %convert_element_type.23.power_ref), custom_call_target="tpu_custom_call" | custom-call | tf_op jit(solution)/shard_map/pallas_call | solution.py:502
  (6 shorter events, 0.1 us)
Async XLA Ops:
  0.0 1.2 %copy-start = (f32[1024,256]{1,0:T(8,128)S(1)}, f32[1024,256]{1,0:T(8,128)}, u32[]{:S(2)}) copy-start(f32[1024,256]{1,0:T(8,128)} %refs_0_.1) | copy-start | bytes 3145732
  2.2 24.1 %copy-start.1 = (bf16[256,768]{1,0:T(8,128)(2,1)S(1)}, bf16[256,768]{1,0:T(8,128)(2,1)}, u32[]{:S(2)}) copy-start(bf16[256,768]{1,0:T(8,128)(2,1)} %constant.27.clone.refs_2_) | copy-start | bytes 1179652
  2.2 24.1 %copy-start.2 = (bf16[256,384]{1,0:T(8,128)(2,1)S(1)}, bf16[256,384]{1,0:T(8,128)(2,1)}, u32[]{:S(2)}) copy-start(bf16[256,384]{1,0:T(8,128)(2,1)} %constant.26.clone.refs_1_) | copy-start | bytes 589828
  2.2 24.1 %copy-start.3 = (f32[2,128,128]{2,1,0:T(8,128)S(1)}, f32[2,128,128]{2,1,0:T(8,128)}, u32[]{:S(2)}) copy-start(f32[2,128,128]{2,1,0:T(8,128)} %constant.29.clone.refs_4_) | copy-start | bytes 393220
  2.2 24.1 %copy-start.4 = (f32[2,128,128]{2,1,0:T(8,128)S(1)}, f32[2,128,128]{2,1,0:T(8,128)}, u32[]{:S(2)}) copy-start(f32[2,128,128]{2,1,0:T(8,128)} %constant.28.clone.refs_3_) | copy-start | bytes 393220
  30.2 4.5 %copy-start.5 = (bf16[16,2,128]{2,1,0:T(2,128)(2,1)S(1)}, bf16[16,2,128]{2,1,0:T(2,128)(2,1)}, u32[]{:S(2)}) copy-start(bf16[16,2,128]{2,1,0:T(2,128)(2,1)} %taps_ref.1) | copy-start | bytes 24580
  31.1 18.4 %all-to-all-start.1 = ((f16[16,136,128]{2,1,0:T(8,128)(2,1)}), f16[16,136,128]{2,1,0:T(8,128)(2,1)S(1)}, u32[]{:S(2)}, u32[]{:S(2)}) async-start(f16[16,136,128]{2,1,0:T(8,128)(2,1)} %convert_element_type.20), calls=%async_computation.1 | async-start | bytes 1114112 | tf_op jit(solution)/shard_map/all_to_all | solution.py:512
  39.5 10.0 %copy-start.6 = (s32[16]{0:T(128)S(1)}, s32[16]{0:T(128)}, u32[]{:S(2)}) copy-start(s32[16]{0:T(128)} %drift_ref.1) | copy-start | bytes 196

commit v5 on v4

--- a/solution.py
+++ b/solution.py
@@ -184,10 +184,11 @@
             high = block.astype(BF16)
             low = (block - high.astype(F32)).astype(BF16)
             cols = slice(part * LANES, (part + 1) * LANES)
-            rhs[0:LANES, cols] = high
-            rhs[LANES : 2 * LANES, cols] = low
-            rhs[2 * LANES : 3 * LANES, cols] = high
-        first = jnp.dot(w1_ref[...], rhs[...], preferred_element_type=F32)
+            rhs[pair, 0:LANES, cols] = high
+            rhs[pair, LANES : 2 * LANES, cols] = low
+            rhs[pair, 2 * LANES : 3 * LANES, cols] = high
+    for pair in range(inner // 2):
+        first = jnp.dot(w1_ref[...], rhs[pair], preferred_element_type=F32)
         for part in range(2):
             cols = slice(part * LANES, (part + 1) * LANES)
             turned = times(
@@ -198,11 +199,12 @@
                 high = turned[comp].astype(BF16)
                 low = (turned[comp] - high.astype(F32)).astype(BF16)
                 at = comp * LANES
-                lhs[rows, at : at + LANES] = high
-                lhs[rows, 2 * LANES + at : 3 * LANES + at] = low
-                lhs[rows, 4 * LANES + at : 5 * LANES + at] = high
+                lhs[pair, rows, at : at + LANES] = high
+                lhs[pair, rows, 2 * LANES + at : 3 * LANES + at] = low
+                lhs[pair, rows, 4 * LANES + at : 5 * LANES + at] = high
+    for pair in range(inner // 2):
         second = lax.dot_general(
-            w2_ref[...], lhs[...], (((1,), (1,)), ((), ())), preferred_element_type=F32
+            w2_ref[...], lhs[pair], (((1,), (1,)), ((), ())), preferred_element_type=F32
         )
         mid[2 * pair] = second[:, :LANES]
         mid[2 * pair + 1] = second[:, LANES:]
@@ -251,8 +253,8 @@
         out_specs=(VMEM_SPEC, VMEM_SPEC),
         compiler_params=ROOM,
         scratch_shapes=[
-            pltpu.VMEM((3 * LANES, 2 * LANES), BF16),
-            pltpu.VMEM((2 * LANES, 6 * LANES), BF16),
+            pltpu.VMEM((inner // 2, 3 * LANES, 2 * LANES), BF16),
+            pltpu.VMEM((inner // 2, 2 * LANES, 6 * LANES), BF16),
             pltpu.VMEM((inner, 2 * LANES, LANES), F32),
             pltpu.VMEM((2, total + 16, LANES), F32),
             pltpu.VMEM((4, LANES, LANES), F32),
@@ -286,9 +288,14 @@
         return carry
 
     lax.fori_loop(0, taps_ref.shape[0], build, 0)
-    copy = pltpu.make_async_copy(out_ref, stored_ref.at[pl.ds(0, out_ref.shape[0])], sent)
-    copy.start()
-    copy.wait()
+    copies = [
+        pltpu.make_async_copy(out_ref.at[index], stored_ref.at[index], sent.at[index])
+        for index in range(out_ref.shape[0])
+    ]
+    for copy in copies:
+        copy.start()
+    for copy in copies:
+        copy.wait()
 
 
 def template_matrices(templates):
@@ -300,7 +307,7 @@
         out_specs=pl.BlockSpec(memory_space=pl.ANY),
         scratch_shapes=[
             pltpu.VMEM((count, 4 * LANES, 2 * LANES), BF16),
-            pltpu.SemaphoreType.DMA,
+            pltpu.SemaphoreType.DMA((count,)),
         ],
         compiler_params=WIDE,
         cost_estimate=pl.CostEstimate(
@@ -327,8 +334,13 @@
     w_ref,
     arrived,
 ):
-    fetch = pltpu.make_async_copy(matrices_ref.at[pl.ds(0, w_ref.shape[0])], w_ref, arrived)
-    fetch.start()
+    count = w_ref.shape[0]
+
+    def fetch(index):
+        return pltpu.make_async_copy(matrices_ref.at[index], w_ref.at[index], arrived.at[index])
+
+    for index in range(count):
+        fetch(index).start()
     groups = z_ref.shape[0]
     own = z_ref.shape[1] // 2 - 4
     half = groups // 2
@@ -407,11 +419,11 @@
     pieces = max(1, main // 512)
     edges = [main // pieces * piece for piece in range(pieces)] + [main + groups]
 
-    fetch.wait()
-    count = w_ref.shape[0]
     batch = math.gcd(count, 8)
 
     def template(turn, carry):
+        for member in range(batch):
+            fetch(turn * batch + member).wait()
         for piece in range(pieces):
             rows = slice(edges[piece], edges[piece + 1])
             here, past = None, None
@@ -468,7 +480,7 @@
             pltpu.VMEM((rows, LANES), F32),
             pltpu.VMEM((rows, LANES), F32),
             pltpu.VMEM((drift.shape[0], 4 * LANES, 2 * LANES), BF16),
-            pltpu.SemaphoreType.DMA,
+            pltpu.SemaphoreType.DMA((drift.shape[0],)),
         ],
     )(place, drift, moved, level, table, matrices)
 

time: 73.6 us -> 72.1 us (0.980)
  Pallas kernels: 18.4 us -> 17.1 us
    pallas_call x1, Pallas kernels: 3.87 us -> 2.94 us  [local_transform(): pl.pallas_call(lambda *refs: local_kernel(groups, unit, *refs), out_shape...]
where the time goes in v5:
time: 72.1 us; the launch traced here: 71.7 us
  blocking collectives  38.6 us (54%)
  Pallas kernels  17.1 us (24%)
  waiting for transfers between devices  8.92 us (12%)
  starting transfers between devices  3.58 us (5%)
  local copies, waits for them, and re-layouts  2.17 us (3%)
  other arithmetic  1.19 us (2%)
    all_to_all x2, blocking collectives, exchange(): lax.all_to_all(value.astype(F16), AXES, split_axis=0, concat_axis=0, tile...  38.6 us
    all_to_all x1, waiting for transfers between devices, exchange(): lax.all_to_all(value.astype(F16), AXES, split_axis=0, concat_axis=0, tile...  8.92 us
    pallas_call x1, Pallas kernels, template_powers(): pl.pallas_call(power_kernel, out_shape=jax.ShapeDtypeStruct((groups, own...  7.47 us
    pallas_call x1, Pallas kernels, template_matrices(): pl.pallas_call(matrix_kernel, out_shape=jax.ShapeDtypeStruct((4 * count,...  4.92 us
    all_to_all x1, starting transfers between devices, exchange(): lax.all_to_all(value.astype(F16), AXES, split_axis=0, concat_axis=0, tile...  3.58 us
    pallas_call x1, Pallas kernels, local_transform(): pl.pallas_call(lambda *refs: local_kernel(groups, unit, *refs), out_shape...  2.94 us
  transfers between devices with their start and end apart: 1, of which 1 were waited for; matrix products, arithmetic and copies ran while one was open for 1% of the time, Pallas kernels for 7%

profile of v5, /device:TPU:0, one launch (start us, length us, event | category | flops | bytes accessed | tf_op | source)
XLA Modules:
  0.0 71.7 jit_solution(18281453189627106639)
XLA Ops:
  0.0 1.2 %copy-done = f32[1024,256]{1,0:T(8,128)S(1)} copy-done((f32[1024,256]{1,0:T(8,128)S(1)}, f32[1024,256]{1,0:T(8,128)}, u32[]{:S(2)}) %copy-start) | copy-done | bytes 1048600
  1.2 0.9 %shard_map.82 = f32[16,136,128]{2,1,0:T(8,128)S(1)} custom-call(f32[1024,256]{1,0:T(8,128)S(1)} %copy-done), custom_call_target="tpu_custom_call" | custom-call | tf_op jit(solution)/shard_map/pallas_call | solution.py:139
  2.1 0.1 convert_element_type.18
  2.2 0.0 copy-start.1
  2.2 0.0 copy-start.2
  2.2 0.0 copy-start.3
  2.2 0.0 copy-start.4
  2.2 24.0 %all_to_all.15 = f16[16,136,128]{2,1,0:T(8,128)(2,1)S(1)} all-to-all(f16[16,136,128]{2,1,0:T(8,128)(2,1)S(1)} %convert_element_type.18), channel_id=1, replica_groups=mesh['band'=2,'gx'=8,'gy'=2] {'gx','gy'}, dimensions={0} | all-to-all | bytes 1114112 | tf_op jit(solution)/shard_map/all_to_all | solution.py:524
  26.2 0.1 convert_element_type.19.refs_0_
  26.3 0.0 copy-done.1
  26.3 0.0 copy-done.2
  26.3 0.0 copy-done.3
  26.4 2.9 %shard_map.83 = (f32[16,136,128]{2,1,0:T(8,128)S(1)}, f32[8,128]{1,0:T(8,128)S(1)}) custom-call(f32[16,136,128]{2,1,0:T(8,128)S(1)} %convert_element_type.19.refs_0_, bf16[256,384]{1,0:T(8,128)(2,1)S(1)} %copy-done.2, bf16[256,768]{1,0:T(8,128)(2,1)S(1)} %copy-done.1, f32[2,128,128]{2,1,0:T(8,128)S(1)} %copy-done.4, f32[2,128,128]{2,1,0:T(8,128)S(1)} %copy-done.3), custom_call_target="tpu_custom_call" | custom-call | tf_op jit(solution)/shard_map/pallas_call | solution.py:246
  29.3 0.0 copy-start.5
  29.3 0.9 %convert_element_type.20 = f16[16,136,128]{2,1,0:T(8,128)(2,1)} convert(f32[16,136,128]{2,1,0:T(8,128)S(1)} %get-tuple-element.7) | non-fusion elementwise | flops 278528 | bytes 1671168 | tf_op jit(solution)/shard_map/convert_element_type | solution.py:524
  30.2 3.6 %all-to-all-start.1 = ((f16[16,136,128]{2,1,0:T(8,128)(2,1)}), f16[16,136,128]{2,1,0:T(8,128)(2,1)S(1)}, u32[]{:S(2)}, u32[]{:S(2)}) async-start(f16[16,136,128]{2,1,0:T(8,128)(2,1)} %convert_element_type.20), calls=%async_computation.1 | async-start | bytes 1114112 | tf_op jit(solution)/shard_map/all_to_all | solution.py:524
  33.8 4.9 %shard_map.84.matrices_ref = bf16[64,512,256]{2,1,0:T(8,128)(2,1)} custom-call(bf16[16,2,128]{2,1,0:T(2,128)(2,1)S(1)} %copy-done.5), custom_call_target="tpu_custom_call" | custom-call | flops 10485760 | bytes 6291456 | tf_op jit(solution)/shard_map/pallas_call | solution.py:303
  38.7 0.0 copy-start.6
  38.7 0.9 %constant_dynamic-slice_fusion.table_ref = f32[2,80,128]{2,1,0:T(8,128)S(1)} fusion(f32[2,1040,128]{2,1,0:T(8,128)} %constant.30.clone, s32[]{:T(128)S(6)} %select_n.3), kind=kLoop, calls=%fused_computation | loop fusion | bytes 163844 | tf_op jit(solution)/shard_map/dynamic_slice | solution.py:543
  39.6 8.9 %all-to-all-done.1 = f16[16,136,128]{2,1,0:T(8,128)(2,1)S(1)} async-done(((f16[16,136,128]{2,1,0:T(8,128)(2,1)}), f16[16,136,128]{2,1,0:T(8,128)(2,1)S(1)}, u32[]{:S(2)}, u32[]{:S(2)}) %all-to-all-start.1) | async-done | bytes 557088 | tf_op jit(solution)/shard_map/all_to_all | solution.py:524
  48.6 0.1 convert_element_type.21.z_ref
  48.6 7.5 %shard_map.85 = f32[16,72,128]{2,1,0:T(8,128)S(1)} custom-call(s32[1]{0:T(128)} %bitcast.place_ref, s32[16]{0:T(128)S(1)} %copy-done.6, f32[16,136,128]{2,1,0:T(8,128)S(1)} %convert_element_type.21.z_ref, f32[8,128]{1,0:T(8,128)S(1)} %get-tuple-element.8.level_ref, f32[2,80,128]{2,1,0:T(8,128)S(1)} %constant_dynamic-slice_fusion.table_ref, ...), custom_call_target="tpu_custom_call" | custom-call | tf_op jit(solution)/shard_map/pallas_call | solution.py:470
  56.2 14.6 %all_to_all.16 = f16[16,72,128]{2,1,0:T(8,128)(2,1)S(1)} all-to-all(f16[16,72,128]{2,1,0:T(8,128)(2,1)S(1)} %convert_element_type.22), channel_id=1, replica_groups=mesh['band'=2,'gx'=8,'gy'=2] {'gx','gy'}, dimensions={0} | all-to-all | bytes 589824 | tf_op jit(solution)/shard_map/all_to_all | solution.py:524
  70.8 0.9 %shard_map.86 = f32[1024,128]{1,0:T(8,128)} custom-call(s32[1]{0:T(128)} %bitcast.place_ref, f32[16,72,128]{2,1,0:T(8,128)S(1)} %convert_element_type.23.power_ref), custom_call_target="tpu_custom_call" | custom-call | tf_op jit(solution)/shard_map/pallas_call | solution.py:514
  (6 shorter events, 0.1 us)
Async XLA Ops:
  0.0 1.2 %copy-start = (f32[1024,256]{1,0:T(8,128)S(1)}, f32[1024,256]{1,0:T(8,128)}, u32[]{:S(2)}) copy-start(f32[1024,256]{1,0:T(8,128)} %refs_0_.1) | copy-start | bytes 3145732
  2.2 24.1 %copy-start.1 = (bf16[256,768]{1,0:T(8,128)(2,1)S(1)}, bf16[256,768]{1,0:T(8,128)(2,1)}, u32[]{:S(2)}) copy-start(bf16[256,768]{1,0:T(8,128)(2,1)} %constant.27.clone.refs_2_) | copy-start | bytes 1179652
  2.2 24.1 %copy-start.2 = (bf16[256,384]{1,0:T(8,128)(2,1)S(1)}, bf16[256,384]{1,0:T(8,128)(2,1)}, u32[]{:S(2)}) copy-start(bf16[256,384]{1,0:T(8,128)(2,1)} %constant.26.clone.refs_1_) | copy-start | bytes 589828
  2.2 24.1 %copy-start.3 = (f32[2,128,128]{2,1,0:T(8,128)S(1)}, f32[2,128,128]{2,1,0:T(8,128)}, u32[]{:S(2)}) copy-start(f32[2,128,128]{2,1,0:T(8,128)} %constant.29.clone.refs_4_) | copy-start | bytes 393220
  2.2 24.1 %copy-start.4 = (f32[2,128,128]{2,1,0:T(8,128)S(1)}, f32[2,128,128]{2,1,0:T(8,128)}, u32[]{:S(2)}) copy-start(f32[2,128,128]{2,1,0:T(8,128)} %constant.28.clone.refs_3_) | copy-start | bytes 393220
  29.3 4.5 %copy-start.5 = (bf16[16,2,128]{2,1,0:T(2,128)(2,1)S(1)}, bf16[16,2,128]{2,1,0:T(2,128)(2,1)}, u32[]{:S(2)}) copy-start(bf16[16,2,128]{2,1,0:T(2,128)(2,1)} %taps_ref.1) | copy-start | bytes 24580
  30.2 18.4 %all-to-all-start.1 = ((f16[16,136,128]{2,1,0:T(8,128)(2,1)}), f16[16,136,128]{2,1,0:T(8,128)(2,1)S(1)}, u32[]{:S(2)}, u32[]{:S(2)}) async-start(f16[16,136,128]{2,1,0:T(8,128)(2,1)} %convert_element_type.20), calls=%async_computation.1 | async-start | bytes 1114112 | tf_op jit(solution)/shard_map/all_to_all | solution.py:524
  38.7 9.9 %copy-start.6 = (s32[16]{0:T(128)S(1)}, s32[16]{0:T(128)}, u32[]{:S(2)}) copy-start(s32[16]{0:T(128)} %drift_ref.1) | copy-start | bytes 196

commit v6 on v5

--- a/solution.py
+++ b/solution.py
@@ -16,7 +16,7 @@
 F16 = jnp.float16
 STEPS = (64, 32, 16, 8, 4, 2, 1)
 PEAK = 2.0**14
-REACH = 2.0**-40
+FLOOR = 1e-30
 ROOM = pltpu.CompilerParams(vmem_limit_bytes=20 * 2**20)
 WIDE = pltpu.CompilerParams(vmem_limit_bytes=50 * 2**20)
 BF16 = jnp.bfloat16
@@ -118,8 +118,11 @@
     rows, width = series_ref.shape
     scale, code = grow(jnp.max(jnp.abs(series_ref[...])), 1.0)
     inner = out_ref.shape[1] - 8
+    energy = jnp.sum(jnp.square(series_ref[...] * (scale / PEAK))) / (rows * width)
+    rank = lax.broadcasted_iota(jnp.int32, (8, LANES), 0)
+    notes = jnp.where(rank < 4, code, energy)
     for dest in range(groups):
-        out_ref[dest, inner : inner + 8, :] = jnp.full((8, LANES), code, F32)
+        out_ref[dest, inner : inner + 8, :] = notes
     per_row = width // groups
     tall = rows // LANES
     for high in range(tall):
@@ -147,7 +150,9 @@
     scale, code = grow(jnp.max(jnp.abs(series)), F32(1.0))
     shaped = (series * scale).reshape(tall, LANES, inner // per_row, per_row, groups)
     moving = jnp.transpose(shaped, (4, 2, 3, 0, 1)).reshape(groups, inner * tall, LANES)
-    return jnp.concatenate([moving, jnp.full((groups, 8, LANES), code, F32)], axis=1)
+    energy = jnp.mean(jnp.square(series * (scale / PEAK)))
+    notes = jnp.where(jnp.arange(8)[None, :, None] < 4, code, energy)
+    return jnp.concatenate([moving, jnp.broadcast_to(notes, (groups, 8, LANES))], axis=1)
 
 
 def local_kernel(
@@ -170,11 +175,14 @@
     taken = y_ref.shape[1] - 8
     tall = taken // inner
     own = out_ref.shape[1] // 2 - 4
-    codes = y_ref[:, taken:, :]
+    codes = jnp.concatenate([y_ref[:, taken : taken + 4, :]] * 2, axis=1)
+    energies = jnp.concatenate([y_ref[:, taken + 4 :, :]] * 2, axis=1)
     least = jnp.min(jnp.min(codes, axis=0), axis=0, keepdims=True)
-    least = jnp.broadcast_to(least, level_ref.shape)
-    level_ref[...] = shrink(least, unit)
+    least = jnp.broadcast_to(least, (8, LANES))
+    level_ref[0] = shrink(least, unit)
     factor = shrink(codes - least[None], 1.0)
+    mean = jnp.sum(energies * (factor * factor), axis=0) * (1.0 / groups)
+    level_ref[1] = jnp.sqrt(mean) * shrink(least, PEAK)
     factor = factor[:, :tall, :] if tall <= 8 else factor[:, :1, :]
     for pair in range(inner // 2):
         for part in range(2):
@@ -247,7 +255,7 @@
         lambda *refs: local_kernel(groups, unit, *refs),
         out_shape=(
             jax.ShapeDtypeStruct((groups, 2 * own + 8, LANES), F32),
-            jax.ShapeDtypeStruct((8, LANES), F32),
+            jax.ShapeDtypeStruct((2, 8, LANES), F32),
         ),
         in_specs=[VMEM_SPEC] * 5,
         out_specs=(VMEM_SPEC, VMEM_SPEC),
@@ -280,11 +288,8 @@
         for part in range(2):
             real, imag = blocks[0][part], blocks[1][part]
             top = slice(part * LANES, (part + 1) * LANES)
-            bottom = slice((2 + part) * LANES, (3 + part) * LANES)
             out_ref[index, top, 0:LANES] = real.astype(BF16)
             out_ref[index, top, LANES:] = imag.astype(BF16)
-            out_ref[index, bottom, 0:LANES] = (-imag).astype(BF16)
-            out_ref[index, bottom, LANES:] = real.astype(BF16)
         return carry
 
     lax.fori_loop(0, taps_ref.shape[0], build, 0)
@@ -302,11 +307,11 @@
     count = templates.shape[0]
     return pl.pallas_call(
         matrix_kernel,
-        out_shape=jax.ShapeDtypeStruct((4 * count, 4 * LANES, 2 * LANES), BF16),
+        out_shape=jax.ShapeDtypeStruct((8 * count, 2 * LANES, 2 * LANES), BF16),
         in_specs=[VMEM_SPEC],
         out_specs=pl.BlockSpec(memory_space=pl.ANY),
         scratch_shapes=[
-            pltpu.VMEM((count, 4 * LANES, 2 * LANES), BF16),
+            pltpu.VMEM((count, 2 * LANES, 2 * LANES), BF16),
             pltpu.SemaphoreType.DMA((count,)),
         ],
         compiler_params=WIDE,
@@ -323,6 +328,7 @@
     drift_ref,
     z_ref,
     level_ref,
+    step_ref,
     table_ref,
     matrices_ref,
     out_ref,
@@ -337,7 +343,8 @@
     count = w_ref.shape[0]
 
     def fetch(index):
-        return pltpu.make_async_copy(matrices_ref.at[index], w_ref.at[index], arrived.at[index])
+        top = w_ref.at[index, pl.ds(0, 2 * LANES), :]
+        return pltpu.make_async_copy(matrices_ref.at[index], top, arrived.at[index])
 
     for index in range(count):
         fetch(index).start()
@@ -424,6 +431,10 @@
     def template(turn, carry):
         for member in range(batch):
             fetch(turn * batch + member).wait()
+        for member in range(batch):
+            index = turn * batch + member
+            w_ref[index, 2 * LANES :, 0:LANES] = -w_ref[index, 0 : 2 * LANES, LANES:]
+            w_ref[index, 2 * LANES :, LANES:] = w_ref[index, 0 : 2 * LANES, 0:LANES]
         for piece in range(pieces):
             rows = slice(edges[piece], edges[piece + 1])
             here, past = None, None
@@ -443,34 +454,29 @@
         return carry
 
     lax.fori_loop(0, count // batch, template, 0)
-    peak = jnp.zeros((8, LANES), F32)
+    gain = jnp.broadcast_to((1.0 / step_ref[...])[0:1, :], (own, LANES))
     for step in range(groups):
         base = step * own
         spare = far[main + step : main + step + 1, :]
         if step < half:
-            dest = 2 * step
-            out_ref[dest, 0:own, :] = near[base : base + own, :] + far[base + 1 : base + own + 1, :]
-            out_ref[dest, own - 1 : own, :] = near[base + own - 1 : base + own, :] + spare
+            dest, edge = 2 * step, own - 1
+            total = near[base : base + own, :] + far[base + 1 : base + own + 1, :]
         else:
-            dest = 2 * (groups - 1 - step) + 1
-            out_ref[dest, 0:own, :] = near[base : base + own, :] + far[base - 1 : base + own - 1, :]
-            out_ref[dest, 0:1, :] = near[base : base + 1, :] + spare
-        for chunk in range(own // 8):
-            peak = jnp.maximum(peak, out_ref[dest, 8 * chunk : 8 * chunk + 8, :])
-    scale, code = grow(jnp.max(peak), REACH)
-    for dest in range(groups):
-        out_ref[dest, 0:own, :] = out_ref[dest, 0:own, :] * scale
-        out_ref[dest, own : own + 8, :] = jnp.full((8, LANES), code, F32)
-
-
-def template_powers(place, drift, moved, level, table, matrices):
+            dest, edge = 2 * (groups - 1 - step) + 1, 0
+            total = near[base : base + own, :] + far[base - 1 : base + own - 1, :]
+        out_ref[dest, :, :] = jnp.sqrt(total) * gain
+        last = near[base + edge : base + edge + 1, :] + spare
+        out_ref[dest, edge : edge + 1, :] = jnp.sqrt(last) * gain[0:1, :]
+
+
+def template_powers(place, drift, moved, level, step, table, matrices):
     groups = moved.shape[0]
     own = moved.shape[1] // 2 - 4
     rows = groups * own + groups
     return pl.pallas_call(
         power_kernel,
-        out_shape=jax.ShapeDtypeStruct((groups, own + 8, LANES), F32),
-        in_specs=[SMEM_SPEC, SMEM_SPEC] + [VMEM_SPEC] * 3 + [pl.BlockSpec(memory_space=pl.ANY)],
+        out_shape=jax.ShapeDtypeStruct((groups, own, LANES), F32),
+        in_specs=[SMEM_SPEC, SMEM_SPEC] + [VMEM_SPEC] * 4 + [pl.BlockSpec(memory_space=pl.ANY)],
         out_specs=VMEM_SPEC,
         compiler_params=WIDE,
         scratch_shapes=[
@@ -482,42 +488,40 @@
             pltpu.VMEM((drift.shape[0], 4 * LANES, 2 * LANES), BF16),
             pltpu.SemaphoreType.DMA((drift.shape[0],)),
         ],
-    )(place, drift, moved, level, table, matrices)
-
-
-def place_kernel(place_ref, power_ref, out_ref):
-    groups, own = power_ref.shape[0], power_ref.shape[1] - 8
+    )(place, drift, moved, level, step, table, matrices)
+
+
+def place_kernel(place_ref, power_ref, step_ref, out_ref):
+    groups, own = power_ref.shape[0], power_ref.shape[1]
     total = groups * own
     flip = 7 - lax.broadcasted_iota(jnp.int32, (8, LANES), 0)
 
     @pl.when(place_ref[0] % 2 == 0)
     def _():
         for source in range(groups):
-            factor = shrink(power_ref[source, own:, :], 1.0 / REACH)
             for chunk in range(own // 8):
                 at = source * own + 8 * chunk
-                value = power_ref[source, 8 * chunk : 8 * chunk + 8, :] * factor
+                value = jnp.square(power_ref[source, 8 * chunk : 8 * chunk + 8, :] * step_ref[...])
                 out_ref[at : at + 8, :] = value
 
     @pl.when(place_ref[0] % 2 == 1)
     def _():
         for source in range(groups):
-            factor = shrink(power_ref[source, own:, :], 1.0 / REACH)
             for chunk in range(own // 8):
                 at = total - source * own - 8 * chunk - 8
-                value = power_ref[source, 8 * chunk : 8 * chunk + 8, :] * factor
+                value = jnp.square(power_ref[source, 8 * chunk : 8 * chunk + 8, :] * step_ref[...])
                 out_ref[at : at + 8, :] = jnp.take_along_axis(value, flip, axis=0)
 
 
-def place_powers(place, moved):
-    groups, own = moved.shape[0], moved.shape[1] - 8
+def place_powers(place, moved, step):
+    groups, own = moved.shape[0], moved.shape[1]
     return pl.pallas_call(
         place_kernel,
         out_shape=jax.ShapeDtypeStruct((groups * own, LANES), F32),
-        in_specs=[SMEM_SPEC, VMEM_SPEC],
+        in_specs=[SMEM_SPEC, VMEM_SPEC, VMEM_SPEC],
         out_specs=VMEM_SPEC,
         compiler_params=ROOM,
-    )(place, moved)
+    )(place, moved, step)
 
 
 def exchange(value):
@@ -548,8 +552,11 @@
     unit = samples / 2 / math.sqrt(length)
     partial, level = local_transform(moved, groups, unit, w1, w2, t1, t2)
     moved = exchange(partial)
-    power = template_powers(place, drift, moved, level, table, matrices)
-    return place_powers(place, exchange(power))
+    taps = 2 * templates.shape[0] * templates.shape[2] ** 2
+    bound = math.sqrt(taps * length) * jnp.max(jnp.abs(templates.astype(F32))) * level[1]
+    step = jnp.maximum(bound, FLOOR) * 2.0**-15
+    power = template_powers(place, drift, moved, level[0], step, table, matrices)
+    return place_powers(place, exchange(power), step)
 
 
 def solution(mesh):

time: 72.1 us -> 71.4 us (level)
  Pallas kernels: 17.1 us -> 16.1 us
    pallas_call x2, Pallas kernels: 12.4 us -> 11.3 us  [the longest x1 7.18 us: template_powers(): pl.pallas_call(power_kernel, out_shape=jax.ShapeDtypeStruct((groups, own,...]
  transfers between devices with their start and end apart: 1 -> 1, of which waited for: 1 -> 1; matrix products, arithmetic and copies ran while one was open for 1% -> 2% of each run, Pallas kernels for 7% -> 6%
where the time goes in v6:
time: 71.4 us; the launch traced here: 71 us
  blocking collectives  38.1 us (53%)
  Pallas kernels  16.1 us (23%)
  waiting for transfers between devices  8.4 us (12%)
  starting transfers between devices  3.58 us (5%)
  local copies, waits for them, and re-layouts  2.17 us (3%)
  other arithmetic  1.81 us (3%)
  between operations  0.82 us (1%)
    all_to_all x2, blocking collectives, exchange(): lax.all_to_all(value.astype(F16), AXES, split_axis=0, concat_axis=0, tile...  38.1 us
    all_to_all x1, waiting for transfers between devices, exchange(): lax.all_to_all(value.astype(F16), AXES, split_axis=0, concat_axis=0, tile...  8.4 us
    pallas_call x1, Pallas kernels, template_powers(): pl.pallas_call(power_kernel, out_shape=jax.ShapeDtypeStruct((groups, own,...  7.18 us
    pallas_call x1, Pallas kernels, template_matrices(): pl.pallas_call(matrix_kernel, out_shape=jax.ShapeDtypeStruct((8 * count,...  4.15 us
    all_to_all x1, starting transfers between devices, exchange(): lax.all_to_all(value.astype(F16), AXES, split_axis=0, concat_axis=0, tile...  3.58 us
    pallas_call x1, Pallas kernels, local_transform(): pl.pallas_call(lambda *refs: local_kernel(groups, unit, *refs), out_shape...  2.97 us
  transfers between devices with their start and end apart: 1, of which 1 were waited for; matrix products, arithmetic and copies ran while one was open for 2% of the time, Pallas kernels for 6%

profile of v6, /device:TPU:0, one launch (start us, length us, event | category | flops | bytes accessed | tf_op | source)
XLA Modules:
  0.0 71.0 jit_solution(12103227374041477121)
XLA Ops:
  0.0 1.2 %copy-done = f32[1024,256]{1,0:T(8,128)S(1)} copy-done((f32[1024,256]{1,0:T(8,128)S(1)}, f32[1024,256]{1,0:T(8,128)}, u32[]{:S(2)}) %copy-start) | copy-done | bytes 1048600
  1.2 1.0 %shard_map.82 = f32[16,136,128]{2,1,0:T(8,128)S(1)} custom-call(f32[1024,256]{1,0:T(8,128)S(1)} %copy-done), custom_call_target="tpu_custom_call" | custom-call | tf_op jit(solution)/shard_map/pallas_call | solution.py:142
  2.2 0.1 convert_element_type.21
  2.3 0.0 copy-start.1
  2.3 0.0 copy-start.2
  2.3 0.0 copy-start.3
  2.3 0.0 copy-start.4
  2.3 24.0 %all_to_all.15 = f16[16,136,128]{2,1,0:T(8,128)(2,1)S(1)} all-to-all(f16[16,136,128]{2,1,0:T(8,128)(2,1)S(1)} %convert_element_type.21), channel_id=1, replica_groups=mesh['band'=2,'gx'=8,'gy'=2] {'gx','gy'}, dimensions={0} | all-to-all | bytes 1114112 | tf_op jit(solution)/shard_map/all_to_all | solution.py:528
  26.3 0.1 convert_element_type.22.refs_0_
  26.4 0.0 copy-done.1
  26.4 0.0 copy-done.2
  26.4 3.0 %shard_map.83 = (f32[16,136,128]{2,1,0:T(8,128)S(1)}, f32[2,8,128]{2,1,0:T(8,128)S(1)}) custom-call(f32[16,136,128]{2,1,0:T(8,128)S(1)} %convert_element_type.22.refs_0_, bf16[256,384]{1,0:T(8,128)(2,1)S(1)} %copy-done.2, bf16[256,768]{1,0:T(8,128)(2,1)S(1)} %copy-done.1, f32[2,128,128]{2,1,0:T(8,128)S(1)} %copy-done.4, f32[2,128,128]{2,1,0:T(8,128)S(1)} %copy-done.3), custom_call_target="tpu_custom_call" | custom-call | tf_op jit(solution)/shard_map/pallas_call | solution.py:254
  29.4 0.0 copy-start.5
  29.4 0.9 %convert_element_type.23 = f16[16,136,128]{2,1,0:T(8,128)(2,1)} convert(f32[16,136,128]{2,1,0:T(8,128)S(1)} %get-tuple-element.7) | non-fusion elementwise | flops 278528 | bytes 1671168 | tf_op jit(solution)/shard_map/convert_element_type | solution.py:528
  30.3 3.6 %all-to-all-start.1 = ((f16[16,136,128]{2,1,0:T(8,128)(2,1)}), f16[16,136,128]{2,1,0:T(8,128)(2,1)S(1)}, u32[]{:S(2)}, u32[]{:S(2)}) async-start(f16[16,136,128]{2,1,0:T(8,128)(2,1)} %convert_element_type.23), calls=%async_computation.1 | async-start | bytes 1114112 | tf_op jit(solution)/shard_map/all_to_all | solution.py:528
  33.9 0.6 abs_reduce_fusion
  35.2 4.2 %shard_map.84.matrices_ref = bf16[128,256,256]{2,1,0:T(8,128)(2,1)} custom-call(bf16[16,2,128]{2,1,0:T(2,128)(2,1)S(1)} %copy-done.5), custom_call_target="tpu_custom_call" | custom-call | flops 10485760 | bytes 6291456 | tf_op jit(solution)/shard_map/pallas_call | solution.py:308
  39.3 0.0 copy-start.6
  39.4 0.9 %constant_dynamic-slice_fusion.table_ref = f32[2,80,128]{2,1,0:T(8,128)S(1)} fusion(f32[2,1040,128]{2,1,0:T(8,128)} %constant.38.clone, s32[]{:T(128)S(6)} %select_n.3), kind=kLoop, calls=%fused_computation.3 | loop fusion | bytes 163844 | tf_op jit(solution)/shard_map/dynamic_slice | solution.py:547
  40.3 8.4 %all-to-all-done.1 = f16[16,136,128]{2,1,0:T(8,128)(2,1)S(1)} async-done(((f16[16,136,128]{2,1,0:T(8,128)(2,1)}), f16[16,136,128]{2,1,0:T(8,128)(2,1)S(1)}, u32[]{:S(2)}, u32[]{:S(2)}) %all-to-all-start.1) | async-done | bytes 557088 | tf_op jit(solution)/shard_map/all_to_all | solution.py:528
  48.7 0.1 convert_element_type.24.z_ref
  48.8 7.2 %shard_map.85 = f32[16,64,128]{2,1,0:T(8,128)S(1)} custom-call(s32[1]{0:T(128)} %bitcast.place_ref, s32[16]{0:T(128)S(1)} %copy-done.6, f32[16,136,128]{2,1,0:T(8,128)S(1)} %convert_element_type.24.z_ref, f32[8,128]{1,0:T(8,128)S(1)} %get-tuple-element.10.level_ref, f32[8,128]{1,0:T(8,128)S(1)} %get-tuple-element.9.step_ref, ...), custom_call_target="tpu_custom_call" | custom-call | tf_op jit(solution)/shard_map/pallas_call | solution.py:476
  56.0 14.1 %all_to_all.16 = f16[16,64,128]{2,1,0:T(8,128)(2,1)S(1)} all-to-all(f16[16,64,128]{2,1,0:T(8,128)(2,1)S(1)} %convert_element_type.26), channel_id=1, replica_groups=mesh['band'=2,'gx'=8,'gy'=2] {'gx','gy'}, dimensions={0} | all-to-all | bytes 524288 | tf_op jit(solution)/shard_map/all_to_all | solution.py:528
  70.1 0.9 %shard_map.86 = f32[1024,128]{1,0:T(8,128)} custom-call(s32[1]{0:T(128)} %bitcast.place_ref, f32[16,64,128]{2,1,0:T(8,128)S(1)} %convert_element_type.27.power_ref, f32[8,128]{1,0:T(8,128)S(1)} %get-tuple-element.9.step_ref), custom_call_target="tpu_custom_call" | custom-call | tf_op jit(solution)/shard_map/pallas_call | solution.py:518
  (8 shorter events, 0.1 us)
Async XLA Ops:
  0.0 1.2 %copy-start = (f32[1024,256]{1,0:T(8,128)S(1)}, f32[1024,256]{1,0:T(8,128)}, u32[]{:S(2)}) copy-start(f32[1024,256]{1,0:T(8,128)} %refs_0_.1) | copy-start | bytes 3145732
  2.3 24.1 %copy-start.1 = (bf16[256,768]{1,0:T(8,128)(2,1)S(1)}, bf16[256,768]{1,0:T(8,128)(2,1)}, u32[]{:S(2)}) copy-start(bf16[256,768]{1,0:T(8,128)(2,1)} %constant.35.clone.refs_2_) | copy-start | bytes 1179652
  2.3 24.1 %copy-start.2 = (bf16[256,384]{1,0:T(8,128)(2,1)S(1)}, bf16[256,384]{1,0:T(8,128)(2,1)}, u32[]{:S(2)}) copy-start(bf16[256,384]{1,0:T(8,128)(2,1)} %constant.34.clone.refs_1_) | copy-start | bytes 589828
  2.3 24.1 %copy-start.3 = (f32[2,128,128]{2,1,0:T(8,128)S(1)}, f32[2,128,128]{2,1,0:T(8,128)}, u32[]{:S(2)}) copy-start(f32[2,128,128]{2,1,0:T(8,128)} %constant.37.clone.refs_4_) | copy-start | bytes 393220
  2.3 24.1 %copy-start.4 = (f32[2,128,128]{2,1,0:T(8,128)S(1)}, f32[2,128,128]{2,1,0:T(8,128)}, u32[]{:S(2)}) copy-start(f32[2,128,128]{2,1,0:T(8,128)} %constant.36.clone.refs_3_) | copy-start | bytes 393220
  29.4 4.5 %copy-start.5 = (bf16[16,2,128]{2,1,0:T(2,128)(2,1)S(1)}, bf16[16,2,128]{2,1,0:T(2,128)(2,1)}, u32[]{:S(2)}) copy-start(bf16[16,2,128]{2,1,0:T(2,128)(2,1)} %taps_ref.1) | copy-start | bytes 24580
  30.3 18.4 %all-to-all-start.1 = ((f16[16,136,128]{2,1,0:T(8,128)(2,1)}), f16[16,136,128]{2,1,0:T(8,128)(2,1)S(1)}, u32[]{:S(2)}, u32[]{:S(2)}) async-start(f16[16,136,128]{2,1,0:T(8,128)(2,1)} %convert_element_type.23), calls=%async_computation.1 | async-start | bytes 1114112 | tf_op jit(solution)/shard_map/all_to_all | solution.py:528
  39.3 9.4 %copy-start.6 = (s32[16]{0:T(128)S(1)}, s32[16]{0:T(128)}, u32[]{:S(2)}) copy-start(s32[16]{0:T(128)} %drift_ref.1) | copy-start | bytes 196
